TPU v7x, 128 devices: a whole 4x4x4 slice. The times are simulated.
128 devices in a mesh: graph: 32 (over y, x, core), dp: 4 (over z).
Axes of the slice: x: 4, y: 4, z: 4, core: 2. Of those that a mesh axis runs over, the one named last changes fastest.
Arguments:
- grid_latent: bfloat16 [4, 16384, 512], P('dp', 'graph'), may hold values from -6 to 6
- mesh_embed: bfloat16 [8192, 512], P('graph'), may hold values from -6 to 6
- mesh_edges: bfloat16 [49152, 512], P('graph'), may hold values from -6 to 6
- edge_geometry: bfloat16 [32, 4, 2048], P('graph'), may hold values from -6 to 6
- edge_counts: int32 [32, 32], P('graph'), may hold values from 0 to 64, as said below
- edge_sources: int32 [32, 2048], P('graph'), may hold values from 0 to 511
- edge_targets: int32 [32, 2048], P('graph'), may hold values from 0 to 255
- halo_sources: int32 [32, 128], P('graph'), may hold values from 0 to 255
- mesh_sources: int32 [32, 1536], P('graph'), may hold values from 0 to 383, as said below
- mesh_targets: int32 [32, 1536], P('graph'), may hold values from 0 to 255
- grid_weight: bfloat16 [512, 512], replicated, may hold values from -0.25 to 0.25
- geometry_weight: float32 [4, 512], replicated, may hold values from -3 to 3
- message_weight: bfloat16 [512, 512], replicated, may hold values from -0.25 to 0.25
- mesh_update: bfloat16 [1024, 512], replicated, may hold values from -0.1875 to 0.1875
- mesh_output: bfloat16 [512, 512], replicated, may hold values from -0.25 to 0.25
- processor: bfloat16 [2, 3584, 512], replicated, may hold values from -0.15625 to 0.15625
- cotangent: bfloat16 [4, 8192, 512], P('dp', 'graph'), may hold values from -6 to 6
Outputs:
- mesh_result: bfloat16 [4, 8192, 512], P('dp', 'graph')
- mesh_gradient: bfloat16 [4, 8192, 512], P('dp', 'graph')
- gradients: bfloat16 [2, 3584, 512], replicated
Inputs may be any that keep to these rules, and one draw needn't show every extreme that they name: Slots of device s for device d beyond edge_counts[s, d] are empty; every device fills all 64 slots for itself, and every device fills all 64 slots for one common device. `edge_sources`: row s holds local grid rows of device s. `edge_targets`: row d holds local mesh rows of device d, for slot c from device s at column s * 64 + c. `halo_sources`: row s, columns d * 4 to d * 4 + 3 are the local rows that device s sends to device d; every device sends 4 rows to every device, itself included. `mesh_sources`: A value under 256 is a local row; a value 256 + s * 4 + k is halo slot k from device s.
All inputs are finite; a program needn't handle non-finite values.
Results may differ from a plain program's by a relative error of at most 0.024.
Values may be sent and summed in bfloat16 or wider, within the bound.
A program may use at most 128 MiB of HBM per device.

v0:
```python
import math

import jax
import jax.numpy as jnp
from jax import lax
from jax.sharding import PartitionSpec as P

EPSILON = 1e-05


def matmul(left, right):
    return jnp.dot(left, right, preferred_element_type=jnp.float32)


def weight_grad(left, right):
    return lax.dot_general(
        left, right, (((0,), (0,)), ((), ())), preferred_element_type=jnp.float32
    )


def input_grad(left, right):
    return lax.dot_general(
        left, right, (((1,), (1,)), ((), ())), preferred_element_type=jnp.float32
    )


def normalize(values):
    center = jnp.mean(values, axis=-1, keepdims=True)
    shifted = values - center
    inverse = lax.rsqrt(jnp.mean(shifted * shifted, axis=-1, keepdims=True) + EPSILON)
    return (shifted * inverse, inverse)


def normalize_back(normed, inverse, upstream):
    first_mean = jnp.mean(upstream, axis=-1, keepdims=True)
    second_mean = jnp.mean(upstream * normed, axis=-1, keepdims=True)
    return inverse * (upstream - first_mean - normed * second_mean)


def swish_slope(values):
    sigma = jax.nn.sigmoid(values)
    return sigma * (1.0 + values * (1.0 - sigma))


def member_table(indices, count_rows, dtype):
    rows_iota = lax.broadcasted_iota(jnp.int32, (count_rows, indices.shape[0]), 0)
    return (rows_iota == indices[None, :]).astype(dtype)


def on_device(
    grid_latent,
    mesh_embed,
    mesh_edges,
    edge_geometry,
    edge_counts,
    edge_sources,
    edge_targets,
    halo_sources,
    mesh_sources,
    mesh_targets,
    grid_weight,
    geometry_weight,
    message_weight,
    mesh_update,
    mesh_output,
    processor,
    cotangent,
):
    width = mesh_embed.shape[1]
    nodes_local = mesh_embed.shape[0]
    peers = lax.axis_size("graph")
    grid_rows = grid_latent[0]
    slots = edge_sources.shape[1]
    capacity = slots // peers
    position = lax.iota(jnp.int32, slots)
    column = position % capacity
    target_peer = position // capacity
    live = column < edge_counts[0][target_peer]
    geometry = edge_geometry[0]
    geometry_term = jnp.einsum("fs,fd->sd", geometry.astype(jnp.float32), geometry_weight)
    grid_proj = matmul(grid_rows, grid_weight)
    messages = jnp.where(
        live[:, None], jax.nn.silu(grid_proj[edge_sources[0]] + geometry_term), 0.0
    ).astype(jnp.bfloat16)
    arrived = lax.all_to_all(messages, "graph", split_axis=0, concat_axis=0, tiled=True)
    hidden_sum = matmul(member_table(edge_targets[0], nodes_local, jnp.bfloat16), arrived).astype(
        jnp.bfloat16
    )
    aggregate = matmul(hidden_sum, message_weight).astype(jnp.bfloat16)
    pre_update = matmul(mesh_embed, mesh_update[:width]) + matmul(aggregate, mesh_update[width:])
    normed_start, inverse_start = normalize(
        matmul(jax.nn.silu(pre_update).astype(jnp.bfloat16), mesh_output)
    )
    nodes = (mesh_embed.astype(jnp.float32) + normed_start).astype(jnp.bfloat16)
    senders = mesh_sources[0]
    receivers = mesh_targets[0]
    halo_index = halo_sources[0]
    extended_rows = nodes_local + halo_index.shape[0]
    recv_table16 = member_table(receivers, nodes_local, jnp.bfloat16)
    edges = mesh_edges
    layers = processor.shape[0]
    stored = []
    for layer_index in range(layers):
        weights = processor[layer_index]
        incoming = lax.all_to_all(
            nodes[halo_index], "graph", split_axis=0, concat_axis=0, tiled=True
        )
        extended = jnp.concatenate([nodes, incoming], 0)
        send_proj = matmul(extended, weights[width : 2 * width])
        recv_proj = matmul(nodes, weights[2 * width : 3 * width])
        pre_edge = matmul(edges, weights[:width]) + send_proj[senders] + recv_proj[receivers]
        hidden_edge = jax.nn.silu(pre_edge).astype(jnp.bfloat16)
        normed_edge, inverse_edge = normalize(matmul(hidden_edge, weights[3 * width : 4 * width]))
        new_edges = (edges.astype(jnp.float32) + normed_edge).astype(jnp.bfloat16)
        summed = matmul(recv_table16, new_edges).astype(jnp.bfloat16)
        pre_node = matmul(nodes, weights[4 * width : 5 * width]) + matmul(
            summed, weights[5 * width : 6 * width]
        )
        hidden_node = jax.nn.silu(pre_node).astype(jnp.bfloat16)
        normed_node, inverse_node = normalize(matmul(hidden_node, weights[6 * width :]))
        new_nodes = (nodes.astype(jnp.float32) + normed_node).astype(jnp.bfloat16)
        stored.append(
            (
                nodes,
                edges,
                pre_edge,
                hidden_edge,
                normed_edge,
                inverse_edge,
                summed,
                pre_node,
                hidden_node,
                normed_node,
                inverse_node,
            )
        )
        nodes, edges = (new_nodes, new_edges)
    scale = 1.0 / math.sqrt(lax.axis_size("dp") * peers * nodes_local)
    grad_nodes = cotangent[0].astype(jnp.float32)
    grad_edges = jnp.zeros(edges.shape, jnp.float32)
    pieces = [None] * layers
    for layer_index in reversed(range(layers)):
        weights = processor[layer_index]
        (
            layer_nodes,
            layer_edges,
            pre_edge,
            hidden_edge,
            normed_edge,
            inverse_edge,
            summed,
            pre_node,
            hidden_node,
            normed_node,
            inverse_node,
        ) = stored[layer_index]
        q_node = normalize_back(normed_node, inverse_node, grad_nodes).astype(jnp.bfloat16)
        grad_node_second = weight_grad(hidden_node, q_node)
        d_node = (input_grad(q_node, weights[6 * width :]) * swish_slope(pre_node)).astype(
            jnp.bfloat16
        )
        grad_node_own = weight_grad(layer_nodes, d_node)
        grad_node_sum = weight_grad(summed, d_node)
        grad_summed = input_grad(d_node, weights[5 * width : 6 * width])
        edge_upstream = grad_edges + grad_summed[receivers]
        q_edge = normalize_back(normed_edge, inverse_edge, edge_upstream).astype(jnp.bfloat16)
        grad_edge_second = weight_grad(hidden_edge, q_edge)
        d_edge = input_grad(q_edge, weights[3 * width : 4 * width]) * swish_slope(pre_edge)
        d_edge16 = d_edge.astype(jnp.bfloat16)
        send_extended = jax.ops.segment_sum(d_edge, senders, num_segments=extended_rows)
        returned = lax.all_to_all(
            send_extended[nodes_local:].astype(jnp.bfloat16),
            "graph",
            split_axis=0,
            concat_axis=0,
            tiled=True,
        ).astype(jnp.float32)
        grad_send = (
            send_extended[:nodes_local]
            + jax.ops.segment_sum(returned, halo_index, num_segments=nodes_local)
        ).astype(jnp.bfloat16)
        grad_recv = jax.ops.segment_sum(d_edge, receivers, num_segments=nodes_local).astype(
            jnp.bfloat16
        )
        partial_value = (
            jnp.concatenate(
                [
                    weight_grad(layer_edges, d_edge16),
                    weight_grad(layer_nodes, grad_send),
                    weight_grad(layer_nodes, grad_recv),
                    grad_edge_second,
                    grad_node_own,
                    grad_node_sum,
                    grad_node_second,
                ],
                0,
            )
            * scale
        )
        grad_edges = edge_upstream + input_grad(d_edge16, weights[:width])
        grad_nodes = (
            grad_nodes
            + input_grad(d_node, weights[4 * width : 5 * width])
            + input_grad(grad_send, weights[width : 2 * width])
            + input_grad(grad_recv, weights[2 * width : 3 * width])
        )
        pieces[layer_index] = lax.psum(partial_value, ("graph", "dp")).astype(jnp.bfloat16)
    gradients = jnp.stack(pieces)
    return (nodes[None], grad_nodes.astype(jnp.bfloat16)[None], gradients)


def solution(mesh):
    in_specs = (
        P("dp", "graph", None),
        P("graph", None),
        P("graph", None),
        P("graph", None, None),
        P("graph", None),
        P("graph", None),
        P("graph", None),
        P("graph", None),
        P("graph", None),
        P("graph", None),
        P(),
        P(),
        P(),
        P(),
        P(),
        P(),
        P("dp", "graph", None),
    )
    out_specs = (P("dp", "graph", None), P("dp", "graph", None), P())
    return jax.shard_map(
        on_device, mesh=mesh, in_specs=in_specs, out_specs=out_specs, check_vma=False
    )
```

profile of v0, /device:TPU:1, one launch (start us, length us, event | category | flops | bytes accessed | tf_op | source)
XLA Modules:
  0.0 447.5 jit_solution(3885011062127873685)
XLA Ops:
  8.0 8.9 %gather_fusion = f32[2048,512]{1,0:T(8,128)} fusion(f32[512,512]{1,0:T(8,128)S(1)} %fusion.73, s32[2048]{0:T(1024)S(1)} %broadcast_clamp_fusion), kind=kCustom, calls=%fused_computation | custom fusion | bytes 8396800 | tf_op jit(solution)/shard_map/gather | solution.py:83
  21.4 15.6 %fusion.129 = pred[2048]{0:T(1024)(128)(4,1)S(1)} fusion(pred[2048]{0:T(1024)(128)(4,1)S(1)} %compare_reduce_fusion, pred[2048]{0:T(1024)(128)(4,1)S(1)} %compare_reduce_fusion.1, pred[2048]{0:T(1024)(128)(4,1)S(1)} %compare_reduce_fusion.2, pred[2048]{0:T(1024)(128)(4,1)S(1)} %compare_reduce_fusion.3, pred[2048]{0:T(1024)(128)(4,1)S(1)} %compare_reduce_fusion.4, ...), kind=kLoop, calls=%fused_computation.251 | loop fusion | flops 65536 | bytes 61540 | tf_op jit(solution)/shard_map/lt | solution.py:78
  41.2 8.8 %all-to-all-start = ((bf16[32,64,512]{2,1,0:T(8,128)(2,1)}), bf16[32,64,512]{2,1,0:T(8,128)(2,1)}, u32[]{:S(2)}, u32[]{:S(2)}) async-start(bf16[32,64,512]{2,1,0:T(8,128)(2,1)} %bitcast.38), calls=%async_computation | async-start | bytes 4194304 | tf_op jit(solution)/shard_map/all_to_all | solution.py:85
  55.1 23.6 %all-to-all-done = bf16[32,64,512]{2,1,0:T(8,128)(2,1)} async-done(((bf16[32,64,512]{2,1,0:T(8,128)(2,1)}), bf16[32,64,512]{2,1,0:T(8,128)(2,1)}, u32[]{:S(2)}, u32[]{:S(2)}) %all-to-all-start) | async-done | bytes 2097184 | tf_op jit(solution)/shard_map/all_to_all | solution.py:85
  86.0 5.8 %all-to-all-start.1 = ((bf16[32,4,512]{2,1,0:T(4,128)(2,1)}), bf16[32,4,512]{2,1,0:T(4,128)(2,1)S(1)}, u32[]{:S(2)}, u32[]{:S(2)}) async-start(bf16[32,4,512]{2,1,0:T(4,128)(2,1)} %all_to_all.39), calls=%async_computation.1 | async-start | bytes 262144 | tf_op jit(solution)/shard_map/all_to_all | solution.py:105
  94.5 4.9 %gather_fusion.3 = f32[1536,512]{1,0:T(8,128)} fusion(f32[256,512]{1,0:T(8,128)S(1)} %fusion.64, s32[2048]{0:T(1024)S(1)} %get-tuple-element.55), kind=kCustom, calls=%fused_computation.3 | custom fusion | bytes 6297600 | tf_op jit(solution)/shard_map/gather | solution.py:111
  100.9 5.0 %gather_fusion.2 = f32[1536,512]{1,0:T(8,128)} fusion(f32[384,512]{1,0:T(8,128)S(1)} %fusion.67, s32[2048]{0:T(1024)S(1)} %get-tuple-element.56), kind=kCustom, calls=%fused_computation.2 | custom fusion | bytes 6297600 | tf_op jit(solution)/shard_map/gather | solution.py:111
  121.8 7.8 %all-to-all-start.2 = ((bf16[32,4,512]{2,1,0:T(4,128)(2,1)}), bf16[32,4,512]{2,1,0:T(4,128)(2,1)S(1)}, u32[]{:S(2)}, u32[]{:S(2)}) async-start(bf16[32,4,512]{2,1,0:T(4,128)(2,1)} %all_to_all.42), calls=%async_computation.2 | async-start | bytes 262144 | tf_op jit(solution)/shard_map/all_to_all | solution.py:105
  131.7 4.9 %gather_fusion.6 = f32[1536,512]{1,0:T(8,128)} fusion(f32[256,512]{1,0:T(8,128)S(1)} %fusion.44, s32[2048]{0:T(1024)S(1)} %get-tuple-element.55), kind=kCustom, calls=%fused_computation.6 | custom fusion | bytes 6297600 | tf_op jit(solution)/shard_map/gather | solution.py:111
  138.5 5.0 %gather_fusion.5 = f32[1536,512]{1,0:T(8,128)} fusion(f32[384,512]{1,0:T(8,128)S(1)} %fusion.47, s32[2048]{0:T(1024)S(1)} %copy-done.55), kind=kCustom, calls=%fused_computation.5 | custom fusion | bytes 6297600 | tf_op jit(solution)/shard_map/gather | solution.py:111
  159.3 4.9 %gather_fusion.7 = f32[1536,512]{1,0:T(8,128)} fusion(f32[256,512]{1,0:T(8,128)S(1)} %fusion.37, s32[2048]{0:T(1024)S(1)} %get-tuple-element.55), kind=kCustom, calls=%fused_computation.7 | custom fusion | bytes 6297600 | tf_op jit(solution)/shard_map/gather | solution.py:165
  181.7 10.6 %scatter_custom_fusion = f32[384,512]{1,0:T(8,128)S(1)} fusion(s32[1536]{0:T(1024)} %reduce.30, f32[1536,512]{1,0:T(8,128)} %copy-done.31, f32[]{:T(128)} %constant.79.clone.1), kind=kCustom, calls=%fused_computation.193 | custom fusion | flops 786432 | bytes 786944 | tf_op jit(solution)/shard_map/scatter-add | solution.py:170
  193.0 7.0 %all-to-all-start.3 = ((bf16[32,4,512]{2,1,0:T(4,128)(2,1)}), bf16[32,4,512]{2,1,0:T(4,128)(2,1)S(1)}, u32[]{:S(2)}, u32[]{:S(2)}) async-start(bf16[32,4,512]{2,1,0:T(4,128)(2,1)} %all_to_all.45), calls=%async_computation.3 | async-start | bytes 262144 | tf_op jit(solution)/shard_map/all_to_all | solution.py:171
  201.5 10.4 %scatter_custom_fusion.2 = f32[256,512]{1,0:T(8,128)S(1)} fusion(s32[1536]{0:T(1024)S(1)} %copy-done.58, f32[1536,512]{1,0:T(8,128)} %copy-done.31, f32[]{:T(128)} %constant.79.clone.1), kind=kCustom, calls=%fused_computation.200 | custom fusion | flops 786432 | bytes 524800 | tf_op jit(solution)/shard_map/scatter-add | solution.py:182
  220.1 5.4 %gather_fusion.8 = f32[1536,512]{1,0:T(8,128)} fusion(f32[256,512]{1,0:T(8,128)S(1)} %fusion.57, s32[2048]{0:T(1024)S(1)} %get-tuple-element.55), kind=kCustom, calls=%fused_computation.8 | custom fusion | bytes 6297600 | tf_op jit(solution)/shard_map/gather | solution.py:165
  229.1 5.3 %fusion.140 = (f32[1536]{0:T(1024)S(1)}, f32[1536]{0:T(1024)S(1)}, f32[1536,512]{0,1:T(8,128)S(1)}) fusion(f32[1536]{0:T(1024)S(1)} %add_rsqrt_fusion.1, f32[1536,512]{0,1:T(8,128)S(1)} %copy-done.3, f32[1536]{0:T(1024)S(1)} %broadcast_multiply_fusion.7, f32[1536,512]{0,1:T(8,128)} %copy.29, f32[1536,512]{0,1:T(8,128)} %copy-done.4, ...), kind=kOutput, calls=%fused_computation.284 | convolution fusion | flops 811594752 | bytes 16277504 | tf_op jit(solution)/shard_map/dot_general | solution.py:22
  236.6 4.6 %convolution_multiply_fusion = f32[1536,512]{1,0:T(8,128)} fusion(bf16[1536,512]{0,1:T(8,128)(2,1)S(1)} %multiply_convert_fusion, f32[1536,512]{1,0:T(8,128)S(1)} %copy-done.26, bf16[2,3584,512]{2,1,0:T(8,128)(2,1)} %param.32), kind=kOutput, calls=%fused_computation.21 | convolution fusion | flops 811597824 | bytes 8388608 | tf_op jit(solution)/shard_map/dot_general | solution.py:22
  241.2 10.6 %scatter_custom_fusion.3 = f32[384,512]{1,0:T(8,128)S(1)} fusion(s32[1536]{0:T(1024)} %reduce.30, f32[1536,512]{1,0:T(8,128)} %convolution_multiply_fusion, f32[]{:T(128)} %constant.79.clone.1), kind=kCustom, calls=%fused_computation.191 | custom fusion | flops 786432 | bytes 786944 | tf_op jit(solution)/shard_map/scatter-add | solution.py:170
  264.7 7.1 %broadcast_multiply_fusion = f32[3584,512]{1,0:T(8,128)} fusion(f32[3584,512]{1,0:T(8,128)} %convolution_dynamic-update-slice_fusion.3), kind=kLoop, calls=%fused_computation.19 | loop fusion | flops 1835008 | bytes 14680064 | tf_op jit(solution)/shard_map/mul | solution.py:186
  272.5 7.4 %all-to-all-start.4 = ((bf16[32,4,512]{2,1,0:T(4,128)(2,1)}), bf16[32,4,512]{2,1,0:T(4,128)(2,1)S(1)}, u32[]{:S(2)}, u32[]{:S(2)}) async-start(bf16[32,4,512]{2,1,0:T(4,128)(2,1)} %all_to_all.47), calls=%async_computation.4 | async-start | bytes 262144 | tf_op jit(solution)/shard_map/all_to_all | solution.py:171
  281.3 10.4 %scatter_custom_fusion.5 = f32[256,512]{1,0:T(8,128)S(1)} fusion(s32[1536]{0:T(1024)S(1)} %copy-done.58, f32[1536,512]{1,0:T(8,128)} %convolution_multiply_fusion, f32[]{:T(128)} %constant.79.clone.1), kind=kCustom, calls=%fused_computation.198 | custom fusion | flops 786432 | bytes 524800 | tf_op jit(solution)/shard_map/scatter-add | solution.py:182
  306.2 7.0 %broadcast_multiply_fusion.1 = f32[3584,512]{1,0:T(8,128)} fusion(f32[3584,512]{1,0:T(8,128)} %convolution_dynamic-update-slice_fusion.8), kind=kLoop, calls=%fused_computation.20 | loop fusion | flops 1835008 | bytes 14680064 | tf_op jit(solution)/shard_map/mul | solution.py:186
  313.2 127.1 %all-reduce.2 = (bf16[3584,512]{1,0:T(8,128)(2,1)}, bf16[3584,512]{1,0:T(8,128)(2,1)}) all-reduce(f32[3584,512]{1,0:T(8,128)} %broadcast_multiply_fusion, f32[3584,512]{1,0:T(8,128)} %broadcast_multiply_fusion.1), channel_id=1, replica_groups=mesh['graph'=32,'dp'=4] {'graph','dp'}, use_global_device_ids=true, to_apply=%region_25.26 | all-reduce | flops 3670016 | bytes 22020096 | tf_op jit(solution)/shard_map/psum | solution.py:207
  440.3 6.9 %pad_maximum_fusion = bf16[2,3584,512]{2,1,0:T(8,128)(2,1)} fusion(bf16[1,3584,512]{2,1,0:T(8,128)(2,1)} %bitcast.207, bf16[1,3584,512]{2,1,0:T(8,128)(2,1)} %bitcast.208), kind=kLoop, calls=%fused_computation.15 | loop fusion | flops 3670016 | bytes 14680064 | tf_op jit(solution)/shard_map/stack | solution.py:208
  (272 shorter events, 130.5 us)
Async XLA Ops:
  8.0 29.0 %copy-start.63 = (bf16[1,4,2048]{2,1,0:T(4,128)(2,1)S(1)}, bf16[1,4,2048]{2,1,0:T(4,128)(2,1)}, u32[]{:S(2)}) copy-start(bf16[1,4,2048]{2,1,0:T(4,128)(2,1)} %param.20) | copy-start | bytes 49156
  8.0 29.0 %copy-start.64 = (f32[4,512]{1,0:T(4,128)S(1)}, f32[4,512]{1,0:T(4,128)}, u32[]{:S(2)}) copy-start(f32[4,512]{1,0:T(4,128)} %param.28) | copy-start | bytes 24580
  41.2 8.8 %copy-start.57 = (s32[1,1536]{1,0:T(1,128)S(1)}, s32[1,1536]{1,0:T(1,128)}, u32[]{:S(2)}) copy-start(s32[1,1536]{1,0:T(1,128)} %param.26) | copy-start | bytes 18436
  41.2 9.5 %copy-start.56 = (s32[1,1536]{1,0:T(1,128)S(1)}, s32[1,1536]{1,0:T(1,128)}, u32[]{:S(2)}) copy-start(s32[1,1536]{1,0:T(1,128)} %param.25) | copy-start | bytes 18436
  41.2 11.8 %copy-start.60 = (s32[1,128]{1,0:T(1,128)S(1)}, s32[1,128]{1,0:T(1,128)}, u32[]{:S(2)}) copy-start(s32[1,128]{1,0:T(1,128)} %param.24) | copy-start | bytes 1540
  41.2 11.9 %copy-start.32 = (bf16[1,256,512]{2,1,0:T(8,128)(2,1)S(1)}, bf16[1,256,512]{2,1,0:T(8,128)(2,1)}, u32[]{:S(2)}) copy-start(bf16[1,256,512]{2,1,0:T(8,128)(2,1)} %param.33) | copy-start | bytes 786436
  41.2 12.6 %copy-start.41 = (bf16[256,512]{1,0:T(8,128)(2,1)S(1)}, bf16[256,512]{1,0:T(8,128)(2,1)}, u32[]{:S(2)}) copy-start(bf16[256,512]{1,0:T(8,128)(2,1)} %param.18) | copy-start | bytes 786436
  41.2 37.5 %all-to-all-start = ((bf16[32,64,512]{2,1,0:T(8,128)(2,1)}), bf16[32,64,512]{2,1,0:T(8,128)(2,1)}, u32[]{:S(2)}, u32[]{:S(2)}) async-start(bf16[32,64,512]{2,1,0:T(8,128)(2,1)} %bitcast.38), calls=%async_computation | async-start | bytes 4194304 | tf_op jit(solution)/shard_map/all_to_all | solution.py:85
  50.0 28.7 %copy-start.65 = (s32[1,2048]{1,0:T(1,128)S(1)}, s32[1,2048]{1,0:T(1,128)}, u32[]{:S(2)}) copy-start(s32[1,2048]{1,0:T(1,128)} %param.23) | copy-start | bytes 24580
  53.0 31.5 %copy-start.59 = (s32[1024]{0:T(1024)}, s32[1024]{0:T(1024)S(1)}, u32[]{:S(2)}) copy-start(s32[1024]{0:T(1024)S(1)} %pad_clamp_fusion.2) | copy-start | bytes 12292
  53.1 47.7 %copy-start.54 = (s32[2048]{0:T(1024)}, s32[2048]{0:T(1024)S(1)}, u32[]{:S(2)}) copy-start(s32[2048]{0:T(1024)S(1)} %get-tuple-element.56) | copy-start | bytes 24580
  86.0 13.4 %all-to-all-start.1 = ((bf16[32,4,512]{2,1,0:T(4,128)(2,1)}), bf16[32,4,512]{2,1,0:T(4,128)(2,1)S(1)}, u32[]{:S(2)}, u32[]{:S(2)}) async-start(bf16[32,4,512]{2,1,0:T(4,128)(2,1)} %all_to_all.39), calls=%async_computation.1 | async-start | bytes 262144 | tf_op jit(solution)/shard_map/all_to_all | solution.py:105
  118.3 18.3 %copy-start.11 = (f32[256,512]{1,0:T(8,128)}, f32[256,512]{1,0:T(8,128)S(1)}, u32[]{:S(2)}) copy-start(f32[256,512]{1,0:T(8,128)S(1)} %get-tuple-element.48) | copy-start | bytes 1572868
  118.7 36.6 %copy-start.5 = (bf16[256,512]{1,0:T(8,128)(2,1)}, bf16[256,512]{1,0:T(8,128)(2,1)S(1)}, u32[]{:S(2)}) copy-start(bf16[256,512]{1,0:T(8,128)(2,1)S(1)} %add_convert_fusion.6) | copy-start | bytes 786436
  121.8 15.3 %all-to-all-start.2 = ((bf16[32,4,512]{2,1,0:T(4,128)(2,1)}), bf16[32,4,512]{2,1,0:T(4,128)(2,1)S(1)}, u32[]{:S(2)}, u32[]{:S(2)}) async-start(bf16[32,4,512]{2,1,0:T(4,128)(2,1)} %all_to_all.42), calls=%async_computation.2 | async-start | bytes 262144 | tf_op jit(solution)/shard_map/all_to_all | solution.py:105
  150.1 7.6 %copy-start.7 = (f32[1536,512]{0,1:T(8,128)}, f32[1536,512]{0,1:T(8,128)S(1)}, u32[]{:S(2)}) copy-start(f32[1536,512]{0,1:T(8,128)S(1)} %get-tuple-element.50) | copy-start | bytes 9437188
  166.6 11.4 %copy-start.4 = (f32[1536,512]{0,1:T(8,128)}, f32[1536,512]{0,1:T(8,128)S(1)}, u32[]{:S(2)}) copy-start(f32[1536,512]{0,1:T(8,128)S(1)} %copy.26) | copy-start | bytes 9437188
  181.7 30.4 %copy-start.61 = (s32[1,128]{1,0:T(1,128)S(1)}, s32[1,128]{1,0:T(1,128)}, u32[]{:S(2)}) copy-start(s32[1,128]{1,0:T(1,128)} %param.24) | copy-start | bytes 1540
  193.0 19.0 %all-to-all-start.3 = ((bf16[32,4,512]{2,1,0:T(4,128)(2,1)}), bf16[32,4,512]{2,1,0:T(4,128)(2,1)S(1)}, u32[]{:S(2)}, u32[]{:S(2)}) async-start(bf16[32,4,512]{2,1,0:T(4,128)(2,1)} %all_to_all.45), calls=%async_computation.3 | async-start | bytes 262144 | tf_op jit(solution)/shard_map/all_to_all | solution.py:171
  236.6 15.2 %copy-start.13 = (bf16[1536,512]{1,0:T(8,128)(2,1)S(1)}, bf16[1536,512]{1,0:T(8,128)(2,1)}, u32[]{:S(2)}) copy-start(bf16[1536,512]{1,0:T(8,128)(2,1)} %param.19) | copy-start | bytes 4718596
  264.7 15.2 %copy-start.18 = (f32[256,512]{1,0:T(8,128)S(1)}, f32[256,512]{1,0:T(8,128)}, u32[]{:S(2)}) copy-start(f32[256,512]{1,0:T(8,128)} %copy-done.17) | copy-start | bytes 1572868
  264.7 15.2 %copy-start.22 = (bf16[256,512]{1,0:T(8,128)(2,1)S(1)}, bf16[256,512]{1,0:T(8,128)(2,1)}, u32[]{:S(2)}) copy-start(bf16[256,512]{1,0:T(8,128)(2,1)} %copy-done.21) | copy-start | bytes 786436
  272.5 19.2 %all-to-all-start.4 = ((bf16[32,4,512]{2,1,0:T(4,128)(2,1)}), bf16[32,4,512]{2,1,0:T(4,128)(2,1)S(1)}, u32[]{:S(2)}, u32[]{:S(2)}) async-start(bf16[32,4,512]{2,1,0:T(4,128)(2,1)} %all_to_all.47), calls=%async_computation.4 | async-start | bytes 262144 | tf_op jit(solution)/shard_map/all_to_all | solution.py:171
  440.3 6.9 %copy-start.1 = (bf16[512,512]{1,0:T(8,128)(2,1)S(1)}, bf16[512,512]{1,0:T(8,128)(2,1)}, u32[]{:S(2)}) copy-start(bf16[512,512]{1,0:T(8,128)(2,1)} %param.27) | copy-start | bytes 1572868
  (47 other events, 168.7 us)
where the time goes:
time: 454 us; the launch traced here: 447 us
  blocking collectives  127 us (28%)
  other arithmetic  102 us (22%)
  matrix products  95.1 us (21%)
  local copies, waits for them, and re-layouts  60.9 us (13%)
  starting transfers between devices  36.7 us (8%)
  waiting for transfers between devices  24 us (5%)
    psum x1, blocking collectives, on_device(): lax.psum(partial_value, ('graph', 'dp')).astype(jnp.bfloat16)  127 us
    dot_general x21, matrix products, matmul(): return jnp.dot(left, right, preferred_element_type=jnp.float32)  38.5 us
    dot_general x13, matrix products, input_grad(): lax.dot_general(left, right, (((1,), (1,)), ((), ())), preferred_element_...  29.1 us
    all_to_all x1, waiting for transfers between devices, on_device(): lax.all_to_all(messages, 'graph', split_axis=0, concat_axis=0, tiled=True)  23.6 us
    dot_general x14, matrix products, weight_grad(): lax.dot_general(left, right, (((0,), (0,)), ((), ())), preferred_element_...  23.4 us
    scatter-add x2, other arithmetic, on_device(): jax.ops.segment_sum(d_edge, senders, num_segments=extended_rows)  21.3 us
    scatter-add x2, other arithmetic, on_device(): jax.ops.segment_sum(d_edge, receivers, num_segments=nodes_local)  20.7 us
    gather x4, local copies, waits for them, and re-layouts, on_device(): edge_upstream = grad_edges + grad_summed[receivers]  16.3 us
  transfers between devices with their start and end apart: 5, of which 2 were waited for; matrix products, arithmetic and copies ran while one was open for 10% of the time, Pallas kernels for 0%

commit v1 on v0

v1 whole, which is shorter than its diff:
```python
import functools
import math

import jax
import jax.numpy as jnp
from jax import lax
from jax.experimental import pallas as pl
from jax.experimental.pallas import tpu as pltpu
from jax.sharding import PartitionSpec as P

EPSILON = 1e-05
F32, BF16 = jnp.float32, jnp.bfloat16
LANES = 128
TILE = 256
WE, WS, WR, E2, PV, PA, N2 = range(7)


def mm(left, right):
    return jnp.dot(left, right, preferred_element_type=F32)


def mm_tn(left, right):
    return lax.dot_general(left, right, (((0,), (0,)), ((), ())), preferred_element_type=F32)


def mm_nt(left, right):
    return lax.dot_general(left, right, (((1,), (1,)), ((), ())), preferred_element_type=F32)


def iota(shape, axis):
    return lax.broadcasted_iota(jnp.int32, shape, axis)


def hot(condition):
    return jnp.where(condition, 1.0, 0.0).astype(BF16)


def sigmoid(x):
    return 0.5 * jnp.tanh(0.5 * x) + 0.5


def normalize(y):
    center = jnp.mean(y, axis=-1, keepdims=True)
    shifted = y - center
    inverse = lax.rsqrt(jnp.mean(shifted * shifted, axis=-1, keepdims=True) + EPSILON)
    return shifted * inverse, inverse


def normalize_back(normed, inverse, upstream):
    first = jnp.mean(upstream, axis=-1, keepdims=True)
    second = jnp.mean(upstream * normed, axis=-1, keepdims=True)
    return inverse * (upstream - first - normed * second)


def rows(start, size):
    return pl.ds(pl.multiple_of(start * size, size), size)


def block(which, width):
    return pl.ds(which * width, width)


def column(row):
    return jnp.transpose(jnp.broadcast_to(row, (LANES, LANES)))


def row_hot(row, width):
    index = column(row)
    lane = iota((LANES, LANES), 1)
    return [hot(index == lane + k * LANES) for k in range(width // LANES)]


def pack(values, tiles):
    count, width = values.shape
    parts = width // LANES
    at, of = iota((count * parts, count), 0), iota((count * parts, count), 1)
    total = None
    for c in range(parts):
        piece = mm(hot(at == of * parts + c), values[:, c * LANES : (c + 1) * LANES])
        total = piece if total is None else total + piece
    tiles[...] = total.astype(BF16)


def unpack(tiles, width):
    parts = width // LANES
    total = tiles.shape[0]
    of, at = iota((total // parts, total), 0), iota((total // parts, total), 1)
    whole = tiles[...]
    return jnp.concatenate(
        [mm(hot(at == of * parts + c), whole).astype(BF16) for c in range(parts)], axis=1
    )


def messages_phase(grid, grid_weight, geometry, geometry_weight, counts, sources, out, proj):
    slots = sources.shape[1]
    peers = counts.shape[1]
    capacity = slots // peers
    grid_rows, width = grid.shape
    proj[...] = mm(grid[...], grid_weight[...]).astype(BF16)
    high = geometry_weight[...].astype(BF16)
    low = (geometry_weight[...] - high.astype(F32)).astype(BF16)
    count16 = jnp.broadcast_to(counts[...].astype(F32), (16, peers)).astype(BF16)

    def step(i, carry):
        at = rows(i, TILE)
        slot = i * TILE + iota((1, TILE), 1)
        owner = (i * TILE + iota((peers, TILE), 1)) // capacity
        limit = mm(count16, hot(owner == iota((peers, TILE), 0)))[:1]
        live = (slot % capacity).astype(F32) < limit
        index = jnp.where(live, sources[:, at], -1)
        shape = jnp.where(live, geometry[:, at].astype(F32), 0.0).astype(BF16)
        table = jnp.concatenate(
            [
                jnp.concatenate(row_hot(index[:, k : k + LANES], grid_rows), axis=1)
                for k in range(0, TILE, LANES)
            ],
            axis=0,
        )
        pre = mm(table, proj[...]) + mm_tn(shape, high) + mm_tn(shape, low)
        out[at, :] = (pre * sigmoid(pre)).astype(BF16)
        return carry

    lax.fori_loop(0, slots // TILE, step, 0)


def tables_phase(senders, receivers, gather, scatter, extended):
    edges = senders.shape[1]
    nodes = gather.shape[1] - extended

    def step(i, carry):
        at = rows(i, LANES)
        send, recv = senders[:, at], receivers[:, at]
        gather[at, :extended] = jnp.concatenate(row_hot(send, extended), axis=1)
        gather[at, extended:] = jnp.concatenate(row_hot(recv, nodes), axis=1)
        scatter[:extended, at] = hot(iota((extended, LANES), 0) == send)
        scatter[extended:, at] = hot(iota((nodes, LANES), 0) == recv)
        return carry

    lax.fori_loop(0, edges // LANES, step, 0)


def halo_send(nodes, halo, tiles):
    picked = jnp.concatenate(
        [
            jnp.concatenate(row_hot(halo[:, k : k + LANES], nodes.shape[0]), axis=1)
            for k in range(0, halo.shape[1], LANES)
        ],
        axis=0,
    )
    pack(mm(picked, nodes).astype(BF16), tiles)


def start_phase(arrived, targets, embed, message_weight, update, output, nodes, total):
    slots = targets.shape[1]
    count, width = embed.shape
    total[...] = jnp.zeros_like(total)

    def step(i, carry):
        at = rows(i, 2 * TILE)
        total[...] += mm(hot(iota((count, 2 * TILE), 0) == targets[:, at]), arrived[at, :])
        return carry

    lax.fori_loop(0, slots // (2 * TILE), step, 0)
    aggregate = mm(total[...].astype(BF16), message_weight[...]).astype(BF16)
    pre = mm(embed[...], update[:width]) + mm(aggregate, update[width:])
    normed, _ = normalize(mm((pre * sigmoid(pre)).astype(BF16), output[...]))
    nodes[...] = (embed[...].astype(F32) + normed).astype(BF16)


def forward_phase(weights, nodes, incoming, edges, gather, scatter, saved, new_nodes, proj, total):
    count, width = nodes.shape
    w = lambda which: weights[block(which, width), :]
    extended = gather.shape[1] - count
    proj[:count] = mm(nodes[...], w(WS)).astype(BF16)
    proj[count:extended] = mm(unpack(incoming, width), w(WS)).astype(BF16)
    proj[extended:] = mm(nodes[...], w(WR)).astype(BF16)
    total[...] = jnp.zeros_like(total)

    def step(i, carry):
        at = rows(i, TILE)
        x = edges[at, :]
        pre = mm(x, w(WE)) + mm(gather[at, :], proj[...])
        s = sigmoid(pre)
        act = pre * s
        hid = act.astype(BF16)
        saved["hid"][at, :] = hid
        saved["slope"][at, :] = (s + act * (1.0 - s)).astype(BF16)
        normed, inverse = normalize(mm(hid, w(E2)))
        saved["normed"][at, :] = normed.astype(BF16)
        saved["inverse"][at, :] = jnp.broadcast_to(inverse, (TILE, LANES))
        new = (x.astype(F32) + normed).astype(BF16)
        if saved["edges"] is not None:
            saved["edges"][at, :] = new
        total[...] += mm(scatter[extended:, at], new)
        return carry

    lax.fori_loop(0, edges.shape[0] // TILE, step, 0)
    summed = total[...].astype(BF16)
    pre = mm(nodes[...], w(PV)) + mm(summed, w(PA))
    s = sigmoid(pre)
    act = pre * s
    hid = act.astype(BF16)
    normed, inverse = normalize(mm(hid, w(N2)))
    new_nodes[...] = (nodes[...].astype(F32) + normed).astype(BF16)
    saved["summed"][...] = summed
    saved["node_hid"][...] = hid
    saved["node_slope"][...] = s + act * (1.0 - s)
    saved["node_normed"][...] = normed
    saved["node_inverse"][...] = jnp.broadcast_to(inverse, (count, LANES))


def backward_phase(
    scale, weights, nodes, edges, gather, scatter, saved, grad_nodes, grad_edges, first, last,
    grads, tiles, send, proj, total, acc,
):
    count, width = nodes.shape
    w = lambda which: weights[block(which, width), :]
    extended = gather.shape[1] - count
    upstream = grad_nodes[...]
    q = normalize_back(saved["node_normed"][...], saved["node_inverse"][:, :1], upstream)
    q = q.astype(BF16)

    def put(which, value):
        grads[block(which, width), :] = (value * scale).astype(BF16)

    put(N2, mm_tn(saved["node_hid"][...], q))
    d_node = (mm_nt(q, w(N2)) * saved["node_slope"][...]).astype(BF16)
    put(PV, mm_tn(nodes[...], d_node))
    put(PA, mm_tn(saved["summed"][...], d_node))
    proj[extended:] = mm_nt(d_node, w(PA)).astype(BF16)
    grad_nodes[...] = upstream + mm_nt(d_node, w(PV))
    total[...] = jnp.zeros_like(total)
    acc[...] = jnp.zeros_like(acc)

    def step(i, carry):
        at = rows(i, TILE)
        up = mm(gather[at, extended:], proj[extended:])
        if not first:
            up = up + grad_edges[at, :]
        q = normalize_back(saved["normed"][at, :].astype(F32), saved["inverse"][at, :1], up)
        q = q.astype(BF16)
        acc[width:] += mm_tn(saved["hid"][at, :], q)
        d = (mm_nt(q, w(E2)) * saved["slope"][at, :].astype(F32)).astype(BF16)
        acc[:width] += mm_tn(edges[at, :], d)
        total[...] += mm(scatter[:, at], d)
        if not last:
            grad_edges[at, :] = up + mm_nt(d, w(WE))
        return carry

    lax.fori_loop(0, edges.shape[0] // TILE, step, 0)
    put(WE, acc[:width])
    put(E2, acc[width:])
    pack(total[count:extended].astype(BF16), tiles)
    send[...] = total[:count]
    recv = total[extended:].astype(BF16)
    put(WR, mm_tn(nodes[...], recv))
    grad_nodes[...] += mm_nt(recv, w(WR))


def finish_phase(scale, weights, nodes, returned, halo, send, grad_nodes, put):
    count, width = nodes.shape
    back = hot(iota((count, halo.shape[1]), 0) == halo[...])
    total = (send[...] + mm(back, unpack(returned, width))).astype(BF16)
    put((mm_tn(nodes[...], total) * scale).astype(BF16))
    grad_nodes[...] += mm_nt(total, weights[block(WS, width), :])


SAVED = ("hid", "slope", "normed", "inverse", "edges", "summed", "node_hid", "node_slope", "node_normed", "node_inverse")


def saved_shapes(edges, nodes, width, with_edges):
    shapes = {
        "hid": ((edges, width), BF16),
        "slope": ((edges, width), BF16),
        "normed": ((edges, width), BF16),
        "inverse": ((edges, LANES), F32),
        "edges": ((edges, width), BF16),
        "summed": ((nodes, width), BF16),
        "node_hid": ((nodes, width), BF16),
        "node_slope": ((nodes, width), F32),
        "node_normed": ((nodes, width), F32),
        "node_inverse": ((nodes, LANES), F32),
    }
    return [shapes[name] for name in SAVED if with_edges or name != "edges"]


def saved_refs(refs, with_edges):
    names = [name for name in SAVED if with_edges or name != "edges"]
    found = dict(zip(names, refs))
    found.setdefault("edges", None)
    return found


def call(kernel, args, outs, scratch=(), aliases=None):
    vmem = pl.BlockSpec(memory_space=pltpu.VMEM)
    return pl.pallas_call(
        kernel,
        out_shape=[jax.ShapeDtypeStruct(*out) for out in outs],
        in_specs=[vmem] * len(args),
        out_specs=[vmem] * len(outs),
        scratch_shapes=[pltpu.VMEM(*s) for s in scratch],
        input_output_aliases=aliases or {},
    )(*args)


def on_device(
    grid_latent,
    mesh_embed,
    mesh_edges,
    edge_geometry,
    edge_counts,
    edge_sources,
    edge_targets,
    halo_sources,
    mesh_sources,
    mesh_targets,
    grid_weight,
    geometry_weight,
    message_weight,
    mesh_update,
    mesh_output,
    processor,
    cotangent,
):
    count, width = mesh_embed.shape
    edges = mesh_edges.shape[0]
    slots = edge_sources.shape[1]
    halo = halo_sources.shape[1]
    peers = lax.axis_size("graph")
    grid_rows = grid_latent.shape[1]
    extended = count + halo
    table = extended + count
    parts = width // LANES
    tiles = (halo * parts, LANES)
    scale = 1.0 / math.sqrt(lax.axis_size("dp") * peers * count)
    exchange = lambda values: lax.all_to_all(
        values.reshape(peers, -1, values.shape[-1]), "graph", split_axis=0, concat_axis=0, tiled=True
    ).reshape(values.shape)

    (messages,) = call(
        lambda *refs: messages_phase(*refs),
        (grid_latent[0], grid_weight, edge_geometry[0], geometry_weight, edge_counts, edge_sources),
        [((slots, width), BF16)],
        [((grid_rows, width), BF16)],
    )
    arrived = exchange(messages)
    gather, scatter = call(
        lambda *refs: tables_phase(*refs, extended),
        (mesh_sources, mesh_targets),
        [((edges, table), BF16), ((table, edges), BF16)],
    )

    def begin(arrived, targets, embed, message_weight, update, output, halo, nodes, out, total):
        start_phase(arrived, targets, embed, message_weight, update, output, nodes, total)
        halo_send(nodes[...], halo, out)

    nodes0, out = call(
        begin,
        (arrived, edge_targets, mesh_embed, message_weight, mesh_update, mesh_output, halo_sources),
        [((count, width), BF16), (tiles, BF16)],
        [((count, width), F32)],
    )
    incoming = exchange(out)
    wide = [((table, width), BF16), ((count, width), F32)]

    def layer0(weights, nodes, incoming, edges, gather, scatter, halo, new_nodes, out, *rest):
        saved = saved_refs(rest[:-2], True)
        forward_phase(weights, nodes, incoming, edges, gather, scatter, saved, new_nodes, *rest[-2:])
        halo_send(new_nodes[...], halo, out)

    nodes1, out, *saved0 = call(
        layer0,
        (processor[0], nodes0, incoming, mesh_edges, gather, scatter, halo_sources),
        [((count, width), BF16), (tiles, BF16), *saved_shapes(edges, count, width, True)],
        wide,
    )
    incoming = exchange(out)
    edges1 = saved0[SAVED.index("edges")]
    grads_shape = ((7 * width, width), BF16)
    work = [
        ((table, width), BF16),
        ((table, width), F32),
        ((2 * width, width), F32),
    ]
    n_saved = len(SAVED) - 1

    def layer1(
        weights, nodes, incoming, edges, gather, scatter, cot, new_nodes, grads, tiles, send,
        grad_nodes, grad_edges, *rest,
    ):
        saved = saved_refs(rest[:n_saved], False)
        total_f, proj, total, acc = rest[n_saved:]
        forward_phase(weights, nodes, incoming, edges, gather, scatter, saved, new_nodes, proj, total_f)
        grad_nodes[...] = cot[...].astype(F32)
        grads[block(WS, width), :] = jnp.zeros((width, width), BF16)
        backward_phase(
            scale, weights, nodes, edges, gather, scatter, saved, grad_nodes, grad_edges, True, False,
            grads, tiles, send, proj, total, acc,
        )

    nodes2, grads1, back, send, grad_nodes, grad_edges = call(
        layer1,
        (processor[1], nodes1, incoming, edges1, gather, scatter, cotangent[0]),
        [
            ((count, width), BF16),
            grads_shape,
            (tiles, BF16),
            ((count, width), F32),
            ((count, width), F32),
            ((edges, width), F32),
        ],
        [*saved_shapes(edges, count, width, False), ((count, width), F32), *work],
    )
    returned = exchange(back)

    def middle(
        weights1, nodes1, returned, halo, send1, gn, weights, nodes, edges, gather, scatter, ge, *rest
    ):
        saved = saved_refs(rest[: len(SAVED)], True)
        grads, tiles, send, grad_nodes, proj, total, acc = rest[len(SAVED) :]
        grad_nodes[...] = gn[...]

        def put(value):
            grads[7 * width :, :] = value

        finish_phase(scale, weights1, nodes1, returned, halo, send1, grad_nodes, put)
        backward_phase(
            scale, weights, nodes, edges, gather, scatter, saved, grad_nodes, ge, False, True,
            grads, tiles, send, proj, total, acc,
        )

    grads0, back, send, grad_nodes = call(
        middle,
        (
            processor[1], nodes1, returned, halo_sources, send, grad_nodes, processor[0], nodes0,
            mesh_edges, gather, scatter, grad_edges, *saved0,
        ),
        [
            ((8 * width, width), BF16),
            (tiles, BF16),
            ((count, width), F32),
            ((count, width), F32),
        ],
        work,
    )
    returned = exchange(back)

    def end(weights, nodes, returned, halo, send, gn, last_grad, result, total):
        total[...] = gn[...]

        def put(value):
            last_grad[...] = value

        finish_phase(scale, weights, nodes, returned, halo, send, total, put)
        result[...] = total[...].astype(BF16)

    last0, result = call(
        end,
        (processor[0], nodes0, returned, halo_sources, send, grad_nodes),
        [((width, width), BF16), ((count, width), BF16)],
        [((count, width), F32)],
    )
    whole1 = lax.psum(grads1, ("graph", "dp"))
    grads0 = lax.dynamic_update_slice(grads0, last0, (width, 0))
    grads0, whole1 = lax.optimization_barrier((grads0, whole1))
    whole0 = lax.psum(grads0, ("graph", "dp"))
    whole1 = lax.dynamic_update_slice(whole1, whole0[7 * width :], (width, 0))
    gradients = jnp.stack([whole0[: 7 * width], whole1])
    return nodes2[None], result[None], gradients


def solution(mesh):
    in_specs = (
        P("dp", "graph", None),
        P("graph", None),
        P("graph", None),
        P("graph", None, None),
        P("graph", None),
        P("graph", None),
        P("graph", None),
        P("graph", None),
        P("graph", None),
        P("graph", None),
        P(),
        P(),
        P(),
        P(),
        P(),
        P(),
        P("dp", "graph", None),
    )
    out_specs = (P("dp", "graph", None), P("dp", "graph", None), P())
    return jax.shard_map(
        on_device, mesh=mesh, in_specs=in_specs, out_specs=out_specs, check_vma=False
    )
```

time: 454 us -> 456 us (level); the launches traced: 447 us -> 455 us
  waiting for transfers between devices: 24 us -> 259 us
  other arithmetic: 102 us -> 3.68 us
  matrix products: 95.1 us -> 0 us
  Pallas kernels: 0 us -> 84.4 us
  blocking collectives: 127 us -> 76.1 us
  local copies, waits for them, and re-layouts: 60.9 us -> 14.2 us
  starting transfers between devices: 36.7 us -> 3.99 us
  between operations: 2.12 us -> 14.1 us
    psum x0 -> x2, waiting for transfers between devices: none -> 259 us  [the longest x1 158 us: on_device(): whole0 = lax.psum(grads0, ('graph', 'dp'))]
    psum x1 -> x0, blocking collectives: 127 us -> none  [on_device(): lax.psum(partial_value, ('graph', 'dp')).astype(jnp.bfloat16)]
    dot_general x49 -> x0, matrix products: 95.1 us -> none  [the longest x21 38.5 us: matmul(): return jnp.dot(left, right, preferred_element_type=jnp.float32)]
    pallas_call x0 -> x7, Pallas kernels: none -> 84.4 us  [call(): pl.pallas_call(kernel, out_shape=[jax.ShapeDtypeStruct(*out) for out in o...]
    all_to_all x0 -> x4, blocking collectives: none -> 76.1 us  [on_device(): lax.all_to_all(values.reshape(peers, -1, values.shape[-1]), 'graph', spli...]
    gather x13 -> x0, local copies, waits for them, and re-layouts: 50.7 us -> none  [the longest x4 16.3 us: on_device(): edge_upstream = grad_edges + grad_summed[receivers]]
    scatter-add x6 -> x0, other arithmetic: 45.3 us -> none  [the longest x2 21.3 us: on_device(): jax.ops.segment_sum(d_edge, senders, num_segments=extended_rows)]
    all_to_all x5 -> x1, starting transfers between devices: 36.7 us -> 3.91 us  [on_device(): lax.all_to_all(values.reshape(peers, -1, values.shape[-1]), 'graph', spli...]
  transfers between devices with their start and end apart: 5 -> 3, of which waited for: 2 -> 2; matrix products, arithmetic and copies ran while one was open for 10% -> 2% of each run, Pallas kernels for 0% -> 7%
where the time goes in v1:
time: 456 us; the launch traced here: 455 us
  waiting for transfers between devices  259 us (57%)
  Pallas kernels  84.4 us (19%)
  blocking collectives  76.1 us (17%)
  local copies, waits for them, and re-layouts  14.2 us (3%)
  between operations  14.1 us (3%)
    psum x1, waiting for transfers between devices, on_device(): whole0 = lax.psum(grads0, ('graph', 'dp'))  158 us
    psum x1, waiting for transfers between devices, on_device(): whole1 = lax.psum(grads1, ('graph', 'dp'))  100 us
    pallas_call x7, Pallas kernels, call(): pl.pallas_call(kernel, out_shape=[jax.ShapeDtypeStruct(*out) for out in o...  84.4 us
    all_to_all x4, blocking collectives, on_device(): lax.all_to_all(values.reshape(peers, -1, values.shape[-1]), 'graph', spli...  76.1 us
  transfers between devices with their start and end apart: 3, of which 2 were waited for; matrix products, arithmetic and copies ran while one was open for 2% of the time, Pallas kernels for 7%

profile of v1, /device:TPU:1, one launch (start us, length us, event | category | flops | bytes accessed | tf_op | source)
XLA Modules:
  0.0 455.1 jit_solution(9856442717471357442)
XLA Ops:
  7.2 8.2 %shard_map.184 = bf16[2048,512]{1,0:T(8,128)(2,1)} custom-call(bf16[512,512]{1,0:T(8,128)(2,1)} %bitcast.32, bf16[512,512]{1,0:T(8,128)(2,1)} %refs_1_.2, bf16[4,2048]{1,0:T(4,128)(2,1)} %bitcast.39, f32[4,512]{1,0:T(4,128)} %refs_3_.1, s32[1,32]{1,0:T(1,128)} %refs_4_.1, s32[1,2048]{1,0:T(1,128)} %refs_5_.1), custom_call_target="tpu_custom_call" | custom-call | tf_op jit(solution)/shard_map/pallas_call | solution.py:296
  15.3 37.0 %all_to_all.25 = bf16[32,64,512]{2,1,0:T(8,128)(2,1)} all-to-all(bf16[32,64,512]{2,1,0:T(8,128)(2,1)} %bitcast.27), channel_id=1, replica_groups=mesh['graph'=32,'dp'=4] {'graph'}, dimensions={0} | all-to-all | bytes 4194304 | tf_op jit(solution)/shard_map/all_to_all | solution.py:336
  52.3 5.8 %shard_map.185 = (bf16[256,512]{1,0:T(8,128)(2,1)}, bf16[512,128]{1,0:T(8,128)(2,1)}) custom-call(bf16[2048,512]{1,0:T(8,128)(2,1)} %bitcast.26, s32[1,2048]{1,0:T(1,128)} %targets.1, bf16[256,512]{1,0:T(8,128)(2,1)} %embed.1, bf16[512,512]{1,0:T(8,128)(2,1)} %message_weight.1, bf16[1024,512]{1,0:T(8,128)(2,1)} %update.1, bf16[512,512]{1,0:T(8,128)(2,1)} %output.1, ...), custom_call_target="tpu_custom_call" | custom-call | tf_op jit(solution)/shard_map/pallas_call | solution.py:296
  58.1 3.9 all-to-all-start.1
  62.0 0.0 all-reduce.3.cloned.1.call-start
  62.1 6.6 %slice_bitcast_fusion.1 = (bf16[3584,512]{1,0:T(8,128)(2,1)}, bf16[3584,512]{1,0:T(8,128)(2,1)}) fusion(bf16[2,3584,512]{2,1,0:T(8,128)(2,1)} %param.32), kind=kLoop, calls=%fused_computation.2 | loop fusion | bytes 14680064 | tf_op jit(solution)/shard_map/squeeze | solution.py:373
  68.7 3.9 shard_map.186
  72.6 0.7 copy-done.1
  73.3 14.9 %shard_map.187 = (bf16[256,512]{1,0:T(8,128)(2,1)}, bf16[512,128]{1,0:T(8,128)(2,1)}, bf16[1536,512]{1,0:T(8,128)(2,1)}, bf16[1536,512]{1,0:T(8,128)(2,1)}, bf16...) custom-call(bf16[3584,512]{1,0:T(8,128)(2,1)} %get-tuple-element.63., ...), custom_call_target="tpu_custom_call" | custom-call | tf_op jit(solution)/shard_map/pallas_call | solution.py:296
  88.1 15.2 %all_to_all.26 = bf16[32,16,128]{2,1,0:T(8,128)(2,1)} all-to-all(bf16[32,16,128]{2,1,0:T(8,128)(2,1)} %bitcast.38), channel_id=1, replica_groups=mesh['graph'=32,'dp'=4] {'graph'}, dimensions={0} | all-to-all | bytes 262144 | tf_op jit(solution)/shard_map/all_to_all | solution.py:336
  103.3 25.9 %shard_map.188 = (bf16[256,512]{1,0:T(8,128)(2,1)}, bf16[3584,512]{1,0:T(8,128)(2,1)}, bf16[512,128]{1,0:T(8,128)(2,1)}, f32[256,512]{1,0:T(8,128)}, f32[256,512]{1,0:T(8,128)}, /*index=5*/f32[1536,512]{1,0:T(8,128)}) custom-call(bf16[3584,512]{1,0:T(8,128)(2,1)} %get-tuple-element.64.weights.weights1, bf16[256,512]{1,0:T(8,128)(2,1)} %get-tuple-element.37.nodes.nodes1, ...), custom_call_target="tpu_custom_call" | custom-call | tf_op jit(solution)/shard_map/pallas_call | solution.py:296
  129.3 0.0 all-reduce.5.cloned.1.call-start
  129.3 0.8 copy-done.2
  130.1 11.6 %all_to_all.27 = bf16[32,16,128]{2,1,0:T(8,128)(2,1)} all-to-all(bf16[32,16,128]{2,1,0:T(8,128)(2,1)S(1)} %bitcast.36), channel_id=1, replica_groups=mesh['graph'=32,'dp'=4] {'graph'}, dimensions={0} | all-to-all | bytes 262144 | tf_op jit(solution)/shard_map/all_to_all | solution.py:336
  141.7 21.7 %shard_map.189 = (bf16[4096,512]{1,0:T(8,128)(2,1)}, bf16[512,128]{1,0:T(8,128)(2,1)}, f32[256,512]{1,0:T(8,128)}, f32[256,512]{1,0:T(8,128)}) custom-call(bf16[3584,512]{1,0:T(8,128)(2,1)} %get-tuple-element.64.weights.weights1, bf16[256,512]{1,0:T(8,128)(2,1)} %get-tuple-element.37.nodes.nodes1, bf16[512,128]{1,0:T(8,128)(2,1)} %bitcast.30, ...), custom_call_target="tpu_custom_call" | custom-call | tf_op jit(solution)/shard_map/pallas_call | solution.py:296
  163.5 12.3 %all_to_all.28 = bf16[32,16,128]{2,1,0:T(8,128)(2,1)} all-to-all(bf16[32,16,128]{2,1,0:T(8,128)(2,1)} %bitcast.35), channel_id=1, replica_groups=mesh['graph'=32,'dp'=4] {'graph'}, dimensions={0} | all-to-all | bytes 262144 | tf_op jit(solution)/shard_map/all_to_all | solution.py:336
  175.8 4.1 shard_map.190
  179.8 1.9 constant_dynamic-update-slice_fusion
  181.7 100.5 %all-reduce.3.cloned.1.call-done = bf16[3584,512]{1,0:T(8,128)(2,1)} async-done(((bf16[3584,512]{1,0:T(8,128)(2,1)}), bf16[3584,512]{1,0:T(8,128)(2,1)}) %all-reduce.3.cloned.1.call-update) | async-done | bytes 3670032 | tf_op jit(solution)/shard_map/psum | solution.py:463
  282.2 158.2 %all-reduce.5.cloned.1.call-done = bf16[4096,512]{1,0:T(8,128)(2,1)} async-done(((bf16[4096,512]{1,0:T(8,128)(2,1)}), bf16[4096,512]{1,0:T(8,128)(2,1)}) %all-reduce.5.cloned.1.call-update) | async-done | bytes 4194320 | tf_op jit(solution)/shard_map/psum | solution.py:466
  440.4 2.4 slice_bitcast_fusion
  442.8 0.7 copy-done
  443.5 1.1 fusion
  444.6 3.7 pad_maximum_fusion
  (6 shorter events, 0.0 us)
Async XLA Ops:
  58.1 14.5 %all-to-all-start.1 = ((bf16[32,16,128]{2,1,0:T(8,128)(2,1)}), bf16[32,16,128]{2,1,0:T(8,128)(2,1)S(1)}, u32[]{:S(2)}, u32[]{:S(2)}) async-start(bf16[32,16,128]{2,1,0:T(8,128)(2,1)} %bitcast.37), calls=%async_computation.1 | async-start | bytes 262144 | tf_op jit(solution)/shard_map/all_to_all | solution.py:336
  62.0 220.1 %all-reduce.3.cloned.1.call-start = ((), (), s32[]{:S(2)}) async-start(), calls=%async_computation.5 | async-start | bytes 7340032 | tf_op jit(solution)/shard_map/psum | solution.py:463
  72.6 0.7 copy-start.1
  129.2 0.9 copy-start.2
  129.3 311.1 %all-reduce.5.cloned.1.call-start = ((), (), s32[]{:S(2)}) async-start(), calls=%async_computation.6 | async-start | bytes 8388608 | tf_op jit(solution)/shard_map/psum | solution.py:466
  440.4 3.1 copy-start
Sparse Core Ops, SparseCore 0:
  129.4 152.7 all-reduce.2
  287.7 152.6 all-reduce.4

commit v2 on v1

--- a/solution.py
+++ b/solution.py
@@ -263,6 +263,165 @@
     total = (send[...] + mm(back, unpack(returned, width))).astype(BF16)
     put((mm_tn(nodes[...], total) * scale).astype(BF16))
     grad_nodes[...] += mm_nt(total, weights[block(WS, width), :])
+
+
+class Reducer:
+    def __init__(self, source, result, refs):
+        (self.half_in, self.half, self.quarter_in, self.quarter, self.tile_in, self.sent, self.got) = refs
+        self.source, self.result = source, result
+        graph, dp = lax.axis_index("graph"), lax.axis_index("dp")
+        self.core = lax.rem(graph, 2)
+        self.place = [lax.rem(graph // 2, 4), graph // 8, dp]
+
+    def device(self, core, place):
+        return (place[1] * 8 + place[0] * 2 + core, place[2])
+
+    def partner(self):
+        return self.device(1 - self.core, self.place)
+
+    def along(self, axis, k):
+        place = list(self.place)
+        place[axis] = lax.rem(place[axis] + k, 4)
+        return place[axis], self.device(self.core, place)
+
+    def over(self, axis, k):
+        first, second = [a for a in range(3) if a != axis]
+        where = lax.rem(self.place[first] * 4 + self.place[second] + k, 16)
+        place = list(self.place)
+        place[first], place[second] = where // 4, lax.rem(where, 4)
+        return where, self.device(self.core, place)
+
+    def enter(self):
+        barrier = pltpu.get_barrier_semaphore()
+        pl.semaphore_signal(barrier, inc=1, device_id=self.partner(), device_id_type=pl.DeviceIdType.MESH)
+        for axis in range(3):
+
+            def greet(k, carry):
+                _, device = self.over(axis, k)
+                pl.semaphore_signal(barrier, inc=1, device_id=device, device_id_type=pl.DeviceIdType.MESH)
+                return carry
+
+            lax.fori_loop(1, 16, greet, 0)
+        pl.semaphore_wait(barrier, 46)
+
+    def send(self, b, stage, source, target, device):
+        pltpu.make_async_remote_copy(
+            src_ref=source,
+            dst_ref=target,
+            send_sem=self.sent.at[b, stage],
+            recv_sem=self.got.at[b, stage],
+            device_id=device,
+            device_id_type=pl.DeviceIdType.MESH,
+        ).start()
+
+    def wait(self, semaphores, b, stage):
+        sizes = (
+            self.half_in.at[b], self.quarter_in.at[b], self.tile_in.at[b],
+            self.tile_in.at[b], self.quarter_in.at[b], self.half_in.at[b],
+        )
+        pltpu.make_async_copy(sizes[stage], sizes[stage], semaphores.at[b, stage]).wait()
+
+    def spot(self, where):
+        at = pl.multiple_of((where // 4) * 16, 16)
+        lane = pl.multiple_of(lax.rem(where, 4) * LANES, LANES)
+        return at, lane
+
+    def begin(self, b):
+        start = pl.multiple_of((1 - self.core) * 256, 256)
+        self.send(b, 0, self.source(b).at[pl.ds(start, 256)], self.half_in.at[b], self.partner())
+
+    def step1(self, b):
+        self.wait(self.got, b, 0)
+        start = pl.multiple_of(self.core * 256, 256)
+        mine = self.source(b)[pl.ds(start, 256), :]
+        self.half[b] = (mine.astype(F32) + self.half_in[b].astype(F32)).astype(BF16)
+        for k in range(1, 4):
+            at, device = self.along(b % 3, k)
+            at = pl.multiple_of(at * 64, 64)
+            self.send(b, 1, self.half.at[b, pl.ds(at, 64)], self.quarter_in.at[b, k - 1], device)
+
+    def step2(self, b):
+        self.wait(self.got, b, 1)
+        at = pl.multiple_of(self.place[b % 3] * 64, 64)
+        total = self.half[b, pl.ds(at, 64), :].astype(F32)
+        for k in range(3):
+            total = total + self.quarter_in[b, k].astype(F32)
+        self.quarter[b] = total.astype(BF16)
+
+        def one(k, carry):
+            where, device = self.over(b % 3, k)
+            at, lane = self.spot(where)
+            self.send(b, 2, self.quarter.at[b, pl.ds(at, 16), pl.ds(lane, LANES)], self.tile_in.at[b, k - 1], device)
+            return carry
+
+        lax.fori_loop(1, 16, one, 0)
+
+    def step3(self, b):
+        self.wait(self.got, b, 2)
+        where, _ = self.over(b % 3, 0)
+        at, lane = self.spot(where)
+        total = self.quarter[b, pl.ds(at, 16), pl.ds(lane, LANES)].astype(F32)
+        total = total + jnp.sum(self.tile_in[b].astype(F32), axis=0)
+        base = self.core * 256 + self.place[b % 3] * 64
+        mine = self.result.at[b, pl.ds(pl.multiple_of(base + at, 16), 16), pl.ds(lane, LANES)]
+        mine[...] = total.astype(BF16)
+
+        def one(k, carry):
+            _, device = self.over(b % 3, k)
+            self.send(b, 3, mine, mine, device)
+            return carry
+
+        lax.fori_loop(1, 16, one, 0)
+
+    def step4(self, b):
+        self.wait(self.got, b, 3)
+        base = pl.multiple_of(self.core * 256 + self.place[b % 3] * 64, 64)
+        mine = self.result.at[b, pl.ds(base, 64)]
+        for k in range(1, 4):
+            self.send(b, 4, mine, mine, self.along(b % 3, k)[1])
+
+    def step5(self, b):
+        self.wait(self.got, b, 4)
+        mine = self.result.at[b, pl.ds(pl.multiple_of(self.core * 256, 256), 256)]
+        self.send(b, 5, mine, mine, self.partner())
+
+    def step6(self, b):
+        self.wait(self.got, b, 5)
+
+    def leave(self, b):
+        for stage in range(6):
+            self.wait(self.sent, b, stage)
+
+
+def reducer_scratch(blocks):
+    return [
+        pltpu.VMEM((blocks, 256, 512), BF16),
+        pltpu.VMEM((blocks, 256, 512), BF16),
+        pltpu.VMEM((blocks, 3, 64, 512), BF16),
+        pltpu.VMEM((blocks, 64, 512), BF16),
+        pltpu.VMEM((blocks, 15, 16, LANES), BF16),
+        pltpu.SemaphoreType.DMA((blocks, 6)),
+        pltpu.SemaphoreType.DMA((blocks, 6)),
+    ]
+
+
+def reduce_phase(grads1, grads0, last0, result, *refs):
+    def source(b):
+        layer, which = divmod(b, 7)
+        if layer == 0:
+            return last0 if which == WS else grads0.at[block(which, 512)]
+        return grads0.at[block(7, 512)] if which == WS else grads1.at[block(which, 512)]
+
+    reducer = Reducer(source, result, refs)
+    reducer.enter()
+    blocks = range(14)
+    steps = (
+        reducer.begin, reducer.step1, reducer.step2, reducer.step3, reducer.step4, reducer.step5,
+        reducer.step6, reducer.leave,
+    )
+    for step in steps:
+        for b in blocks:
+            step(b)
 
 
 SAVED = ("hid", "slope", "normed", "inverse", "edges", "summed", "node_hid", "node_slope", "node_normed", "node_inverse")
@@ -460,12 +619,16 @@
         [((width, width), BF16), ((count, width), BF16)],
         [((count, width), F32)],
     )
-    whole1 = lax.psum(grads1, ("graph", "dp"))
-    grads0 = lax.dynamic_update_slice(grads0, last0, (width, 0))
-    grads0, whole1 = lax.optimization_barrier((grads0, whole1))
-    whole0 = lax.psum(grads0, ("graph", "dp"))
-    whole1 = lax.dynamic_update_slice(whole1, whole0[7 * width :], (width, 0))
-    gradients = jnp.stack([whole0[: 7 * width], whole1])
+    vmem = pl.BlockSpec(memory_space=pltpu.VMEM)
+    gradients = pl.pallas_call(
+        reduce_phase,
+        out_shape=jax.ShapeDtypeStruct((14, width, width), BF16),
+        in_specs=[vmem] * 3,
+        out_specs=vmem,
+        scratch_shapes=reducer_scratch(14),
+        compiler_params=pltpu.CompilerParams(collective_id=0, has_side_effects=True),
+    )(grads1, grads0, last0)
+    gradients = gradients.reshape(2, 7 * width, width)
     return nodes2[None], result[None], gradients
 
 

time: 456 us -> 240 us (0.53)
  waiting for transfers between devices: 259 us -> 0.01 us
  Pallas kernels: 84.4 us -> 144 us
  between operations: 14.1 us -> 0.66 us
    psum x2 -> x0, waiting for transfers between devices: 259 us -> none  [the longest x1 158 us: on_device(): whole0 = lax.psum(grads0, ('graph', 'dp'))]
    pallas_call x0 -> x1, Pallas kernels: none -> 60.4 us  [on_device(): pl.pallas_call(reduce_phase, out_shape=jax.ShapeDtypeStruct((14, width, w...]
    unnamed x6 -> x3, local copies, waits for them, and re-layouts: 2.19 us -> 7.26 us
  transfers between devices with their start and end apart: 3 -> 1, of which waited for: 2 -> 0; matrix products, arithmetic and copies ran while one was open for 2% -> 3% of each run, Pallas kernels for 7% -> 2%
where the time goes in v2:
time: 240 us
  Pallas kernels  144 us (60%)
  blocking collectives  76.8 us (32%)
  local copies, waits for them, and re-layouts  13.8 us (6%)
  starting transfers between devices  3.91 us (2%)
    pallas_call x7, Pallas kernels, call(): pl.pallas_call(kernel, out_shape=[jax.ShapeDtypeStruct(*out) for out in o...  84 us
    all_to_all x4, blocking collectives, on_device(): lax.all_to_all(values.reshape(peers, -1, values.shape[-1]), 'graph', spli...  76.8 us
    pallas_call x1, Pallas kernels, on_device(): pl.pallas_call(reduce_phase, out_shape=jax.ShapeDtypeStruct((14, width, w...  60.4 us
    unnamed x3, local copies, waits for them, and re-layouts  7.26 us
    squeeze x1, local copies, waits for them, and re-layouts, on_device(): processor[0]  6.57 us
  transfers between devices with their start and end apart: 1, of which 0 were waited for; matrix products, arithmetic and copies ran while one was open for 3% of the time, Pallas kernels for 2%

profile of v2, /device:TPU:1, one launch (start us, length us, event | category | flops | bytes accessed | tf_op | source)
XLA Modules:
  0.0 239.6 jit_solution(14099724827714704025)
XLA Ops:
  0.6 8.2 %shard_map.184 = bf16[2048,512]{1,0:T(8,128)(2,1)} custom-call(bf16[512,512]{1,0:T(8,128)(2,1)} %bitcast.26, bf16[512,512]{1,0:T(8,128)(2,1)} %refs_1_.2, bf16[4,2048]{1,0:T(4,128)(2,1)} %bitcast.33, f32[4,512]{1,0:T(4,128)} %refs_3_.1, s32[1,32]{1,0:T(1,128)} %refs_4_.1, s32[1,2048]{1,0:T(1,128)} %refs_5_.1), custom_call_target="tpu_custom_call" | custom-call | tf_op jit(solution)/shard_map/pallas_call | solution.py:455
  8.8 37.0 %all_to_all.25 = bf16[32,64,512]{2,1,0:T(8,128)(2,1)} all-to-all(bf16[32,64,512]{2,1,0:T(8,128)(2,1)} %bitcast.22), channel_id=1, replica_groups=mesh['graph'=32,'dp'=4] {'graph'}, dimensions={0} | all-to-all | bytes 4194304 | tf_op jit(solution)/shard_map/all_to_all | solution.py:495
  45.8 5.8 %shard_map.185 = (bf16[256,512]{1,0:T(8,128)(2,1)}, bf16[512,128]{1,0:T(8,128)(2,1)}) custom-call(bf16[2048,512]{1,0:T(8,128)(2,1)} %bitcast.21, s32[1,2048]{1,0:T(1,128)} %targets.1, bf16[256,512]{1,0:T(8,128)(2,1)} %embed.1, bf16[512,512]{1,0:T(8,128)(2,1)} %message_weight.1, bf16[1024,512]{1,0:T(8,128)(2,1)} %update.1, bf16[512,512]{1,0:T(8,128)(2,1)} %output.1, ...), custom_call_target="tpu_custom_call" | custom-call | tf_op jit(solution)/shard_map/pallas_call | solution.py:455
  51.6 3.9 %all-to-all-start.1 = ((bf16[32,16,128]{2,1,0:T(8,128)(2,1)}), bf16[32,16,128]{2,1,0:T(8,128)(2,1)S(1)}, u32[]{:S(2)}, u32[]{:S(2)}) async-start(bf16[32,16,128]{2,1,0:T(8,128)(2,1)} %bitcast.30), calls=%async_computation.1 | async-start | bytes 262144 | tf_op jit(solution)/shard_map/all_to_all | solution.py:495
  55.5 6.6 %slice_bitcast_fusion = (bf16[3584,512]{1,0:T(8,128)(2,1)}, bf16[3584,512]{1,0:T(8,128)(2,1)}) fusion(bf16[2,3584,512]{2,1,0:T(8,128)(2,1)} %param.32), kind=kLoop, calls=%fused_computation | loop fusion | bytes 14680064 | tf_op jit(solution)/shard_map/squeeze | solution.py:532
  62.1 3.8 %shard_map.186 = (bf16[1536,640]{1,0:T(8,128)(2,1)}, bf16[640,1536]{1,0:T(8,128)(2,1)}) custom-call(s32[1,1536]{1,0:T(1,128)} %refs_0_.1, s32[1,1536]{1,0:T(1,128)} %refs_1_.3), custom_call_target="tpu_custom_call" | custom-call | tf_op jit(solution)/shard_map/pallas_call | solution.py:455
  65.9 0.0 all-to-all-done.1
  65.9 0.0 copy-start
  65.9 0.7 copy-done
  66.6 14.8 %shard_map.187 = (bf16[256,512]{1,0:T(8,128)(2,1)}, bf16[512,128]{1,0:T(8,128)(2,1)}, bf16[1536,512]{1,0:T(8,128)(2,1)}, bf16[1536,512]{1,0:T(8,128)(2,1)}, bf16...) custom-call(bf16[3584,512]{1,0:T(8,128)(2,1)} %get-tuple-element.59., ...), custom_call_target="tpu_custom_call" | custom-call | tf_op jit(solution)/shard_map/pallas_call | solution.py:455
  81.4 15.2 %all_to_all.26 = bf16[32,16,128]{2,1,0:T(8,128)(2,1)} all-to-all(bf16[32,16,128]{2,1,0:T(8,128)(2,1)} %bitcast.31), channel_id=1, replica_groups=mesh['graph'=32,'dp'=4] {'graph'}, dimensions={0} | all-to-all | bytes 262144 | tf_op jit(solution)/shard_map/all_to_all | solution.py:495
  96.6 25.9 %shard_map.188 = (bf16[256,512]{1,0:T(8,128)(2,1)}, bf16[3584,512]{1,0:T(8,128)(2,1)}, bf16[512,128]{1,0:T(8,128)(2,1)}, f32[256,512]{1,0:T(8,128)}, f32[256,512]{1,0:T(8,128)}, /*index=5*/f32[1536,512]{1,0:T(8,128)}) custom-call(bf16[3584,512]{1,0:T(8,128)(2,1)} %get-tuple-element.60.weights.weights1, bf16[256,512]{1,0:T(8,128)(2,1)} %get-tuple-element.35.nodes.nodes1, ...), custom_call_target="tpu_custom_call" | custom-call | tf_op jit(solution)/shard_map/pallas_call | solution.py:455
  122.5 12.3 %all_to_all.27 = bf16[32,16,128]{2,1,0:T(8,128)(2,1)} all-to-all(bf16[32,16,128]{2,1,0:T(8,128)(2,1)} %bitcast.32), channel_id=1, replica_groups=mesh['graph'=32,'dp'=4] {'graph'}, dimensions={0} | all-to-all | bytes 262144 | tf_op jit(solution)/shard_map/all_to_all | solution.py:495
  134.8 21.4 %shard_map.189 = (bf16[4096,512]{1,0:T(8,128)(2,1)}, bf16[512,128]{1,0:T(8,128)(2,1)}, f32[256,512]{1,0:T(8,128)}, f32[256,512]{1,0:T(8,128)}) custom-call(bf16[3584,512]{1,0:T(8,128)(2,1)} %get-tuple-element.60.weights.weights1, bf16[256,512]{1,0:T(8,128)(2,1)} %get-tuple-element.35.nodes.nodes1, bf16[512,128]{1,0:T(8,128)(2,1)} %bitcast.24, ...), custom_call_target="tpu_custom_call" | custom-call | tf_op jit(solution)/shard_map/pallas_call | solution.py:455
  156.2 12.3 %all_to_all.28 = bf16[32,16,128]{2,1,0:T(8,128)(2,1)} all-to-all(bf16[32,16,128]{2,1,0:T(8,128)(2,1)} %bitcast.29), channel_id=1, replica_groups=mesh['graph'=32,'dp'=4] {'graph'}, dimensions={0} | all-to-all | bytes 262144 | tf_op jit(solution)/shard_map/all_to_all | solution.py:495
  168.6 4.0 %shard_map.190 = (bf16[512,512]{1,0:T(8,128)(2,1)}, bf16[256,512]{1,0:T(8,128)(2,1)}) custom-call(bf16[3584,512]{1,0:T(8,128)(2,1)} %get-tuple-element.59.weights, bf16[256,512]{1,0:T(8,128)(2,1)} %get-tuple-element.31.nodes, bf16[512,128]{1,0:T(8,128)(2,1)} %bitcast.27, s32[1,128]{1,0:T(1,128)} %halo.7, f32[256,512]{1,0:T(8,128)} %get-tuple-element.53.send, ...), custom_call_target="tpu_custom_call" | custom-call | tf_op jit(solution)/shard_map/pallas_call | solution.py:455
  172.6 60.4 %shard_map.191 = bf16[14,512,512]{2,1,0:T(8,128)(2,1)} custom-call(bf16[3584,512]{1,0:T(8,128)(2,1)} %get-tuple-element.56.grads1, bf16[4096,512]{1,0:T(8,128)(2,1)} %get-tuple-element.57.grads0, bf16[512,512]{1,0:T(8,128)(2,1)} %get-tuple-element.58.last0), custom_call_target="tpu_custom_call" | custom-call | tf_op jit(solution)/shard_map/pallas_call | solution.py:623
  233.0 6.6 %copy.21 = bf16[2,3584,512]{2,1,0:T(8,128)(2,1)} copy(bf16[2,3584,512]{2,1,0:T(8,128)(2,1)} %bitcast.20) | data formatting | bytes 14680064
Async XLA Ops:
  51.6 14.3 %all-to-all-start.1 = ((bf16[32,16,128]{2,1,0:T(8,128)(2,1)}), bf16[32,16,128]{2,1,0:T(8,128)(2,1)S(1)}, u32[]{:S(2)}, u32[]{:S(2)}) async-start(bf16[32,16,128]{2,1,0:T(8,128)(2,1)} %bitcast.30), calls=%async_computation.1 | async-start | bytes 262144 | tf_op jit(solution)/shard_map/all_to_all | solution.py:495
  65.9 0.7 copy-start

commit v3 on v1

v3 whole, which is shorter than its diff:
```python
import functools
import math

import jax
import jax.numpy as jnp
from jax import lax
from jax.experimental import pallas as pl
from jax.experimental.pallas import tpu as pltpu
from jax.sharding import PartitionSpec as P

EPSILON = 1e-05
F32, BF16 = jnp.float32, jnp.bfloat16
LANES = 128
TILE = 256
WE, WS, WR, E2, PV, PA, N2 = range(7)


def mm(left, right):
    return jnp.dot(left, right, preferred_element_type=F32)


def mm_tn(left, right):
    return lax.dot_general(left, right, (((0,), (0,)), ((), ())), preferred_element_type=F32)


def mm_nt(left, right):
    return lax.dot_general(left, right, (((1,), (1,)), ((), ())), preferred_element_type=F32)


def iota(shape, axis):
    return lax.broadcasted_iota(jnp.int32, shape, axis)


def hot(condition):
    return jnp.where(condition, 1.0, 0.0).astype(BF16)


def sigmoid(x):
    return 0.5 * jnp.tanh(0.5 * x) + 0.5


def normalize(y):
    center = jnp.mean(y, axis=-1, keepdims=True)
    shifted = y - center
    inverse = lax.rsqrt(jnp.mean(shifted * shifted, axis=-1, keepdims=True) + EPSILON)
    return shifted * inverse, inverse


def normalize_back(normed, inverse, upstream):
    first = jnp.mean(upstream, axis=-1, keepdims=True)
    second = jnp.mean(upstream * normed, axis=-1, keepdims=True)
    return inverse * (upstream - first - normed * second)


def rows(start, size):
    return pl.ds(pl.multiple_of(start * size, size), size)


def block(which, width):
    return pl.ds(which * width, width)


def column(row):
    return jnp.transpose(jnp.broadcast_to(row, (LANES, LANES)))


def row_hot(row, width):
    index = column(row)
    lane = iota((LANES, LANES), 1)
    return [hot(index == lane + k * LANES) for k in range(width // LANES)]


def pack(values, tiles):
    count, width = values.shape
    parts = width // LANES
    at, of = iota((count * parts, count), 0), iota((count * parts, count), 1)
    total = None
    for c in range(parts):
        piece = mm(hot(at == of * parts + c), values[:, c * LANES : (c + 1) * LANES])
        total = piece if total is None else total + piece
    tiles[...] = total.astype(BF16)


def unpack(tiles, width):
    parts = width // LANES
    total = tiles.shape[0]
    of, at = iota((total // parts, total), 0), iota((total // parts, total), 1)
    whole = tiles[...]
    return jnp.concatenate(
        [mm(hot(at == of * parts + c), whole).astype(BF16) for c in range(parts)], axis=1
    )


AXES = (1, 1, 0, 2, 2, 0, 1, 0, 0, 2, 1, 1, 2, 0)


class Comm:
    def __init__(self, refs):
        (
            self.grads, self.result, self.half_in, self.quarter_in, self.tile_in, self.sent, self.got,
            self.ex_sent, self.ex_got,
        ) = refs
        self.graph, self.dp = lax.axis_index("graph"), lax.axis_index("dp")
        self.core = lax.rem(self.graph, 2)
        self.place = [lax.rem(self.graph // 2, 4), self.graph // 8, self.dp]

    def device(self, core, place):
        return (place[1] * 8 + place[0] * 2 + core, place[2])

    def partner(self):
        return self.device(1 - self.core, self.place)

    def peer(self, k):
        where = lax.rem(self.graph + k, 32)
        return where, (where, self.dp)

    def along(self, axis, k):
        place = list(self.place)
        place[axis] = lax.rem(place[axis] + k, 4)
        return place[axis], self.device(self.core, place)

    def over(self, axis, k):
        first, second = [a for a in range(3) if a != axis]
        where = lax.rem(self.place[first] * 4 + self.place[second] + k, 16)
        place = list(self.place)
        place[first], place[second] = where // 4, lax.rem(where, 4)
        return where, self.device(self.core, place)

    def greet(self):
        barrier = pltpu.get_barrier_semaphore()

        def signal(device):
            pl.semaphore_signal(barrier, inc=1, device_id=device, device_id_type=pl.DeviceIdType.MESH)

        def near(k, carry):
            signal(self.peer(k)[1])
            return carry

        def far(k, carry):
            signal(self.over(0, k)[1])
            signal(self.over(1, k)[1])
            return carry

        lax.fori_loop(1, 32, near, 0)
        lax.fori_loop(1, 16, far, 0)

    def greeted(self):
        pl.semaphore_wait(pltpu.get_barrier_semaphore(), 61)

    def copy(self, source, target, sent, got, device):
        pltpu.make_async_remote_copy(
            src_ref=source,
            dst_ref=target,
            send_sem=sent,
            recv_sem=got,
            device_id=device,
            device_id_type=pl.DeviceIdType.MESH,
        ).start()

    def send(self, b, stage, source, target, device):
        self.copy(source, target, self.sent.at[b, stage], self.got.at[b, stage], device)

    def wait_size(self, size, semaphore):
        pltpu.make_async_copy(size, size, semaphore).wait()

    def wait(self, semaphores, b, stage):
        sizes = (
            self.half_in.at[b], self.quarter_in.at[b], self.tile_in.at[b],
            self.tile_in.at[b], self.quarter_in.at[b], self.half_in.at[b],
        )
        self.wait_size(sizes[stage], semaphores.at[b, stage])

    def spot(self, where):
        at = pl.multiple_of((where // 4) * 16, 16)
        lane = pl.multiple_of(lax.rem(where, 4) * LANES, LANES)
        return at, lane

    def half_rows(self, core):
        return pl.ds(pl.multiple_of(core * 256, 256), 256)

    def quarter_rows(self, at):
        return pl.ds(pl.multiple_of(self.core * 256 + at * 64, 64), 64)

    def own_spot(self, b, k):
        where, device = self.over(AXES[b], k)
        at, lane = self.spot(where)
        base = self.core * 256 + self.place[AXES[b]] * 64
        return (pl.ds(pl.multiple_of(base + at, 16), 16), pl.ds(lane, LANES)), device

    def begin(self, b):
        other = self.half_rows(1 - self.core)
        self.send(b, 0, self.grads.at[b, other], self.half_in.at[b], self.partner())

    def step1(self, b):
        self.wait(self.got, b, 0)
        mine = self.half_rows(self.core)
        self.grads[b, mine, :] = (self.grads[b, mine, :].astype(F32) + self.half_in[b].astype(F32)).astype(BF16)
        for k in range(1, 4):
            at, device = self.along(AXES[b], k)
            self.send(b, 1, self.grads.at[b, self.quarter_rows(at)], self.quarter_in.at[b, k - 1], device)

    def step2(self, b):
        self.wait(self.got, b, 1)
        mine = self.quarter_rows(self.place[AXES[b]])
        total = self.grads[b, mine, :].astype(F32)
        for k in range(3):
            total = total + self.quarter_in[b, k].astype(F32)
        self.grads[b, mine, :] = total.astype(BF16)

        def one(k, carry):
            spot, device = self.own_spot(b, k)
            self.send(b, 2, self.grads.at[b, spot[0], spot[1]], self.tile_in.at[b, k - 1], device)
            return carry

        lax.fori_loop(1, 16, one, 0)

    def step3(self, b):
        self.wait(self.got, b, 2)
        spot, _ = self.own_spot(b, 0)
        total = self.grads[b, spot[0], spot[1]].astype(F32)
        total = total + jnp.sum(self.tile_in[b].astype(F32), axis=0)
        mine = self.result.at[b, spot[0], spot[1]]
        mine[...] = total.astype(BF16)

        def one(k, carry):
            self.send(b, 3, mine, mine, self.over(AXES[b], k)[1])
            return carry

        lax.fori_loop(1, 16, one, 0)

    def step4(self, b):
        self.wait(self.got, b, 3)
        mine = self.result.at[b, self.quarter_rows(self.place[AXES[b]])]
        for k in range(1, 4):
            self.send(b, 4, mine, mine, self.along(AXES[b], k)[1])

    def step5(self, b):
        self.wait(self.got, b, 4)
        mine = self.result.at[b, self.half_rows(self.core)]
        self.send(b, 5, mine, mine, self.partner())

    def step6(self, b):
        self.wait(self.got, b, 5)

    def leave(self, b):
        for stage in range(6):
            self.wait(self.sent, b, stage)

    def run(self, step, blocks):
        for b in blocks:
            (self.begin, self.step1, self.step2, self.step3, self.step4, self.step5, self.step6)[step](b)

    def exchange(self, e, out, into):
        mine = pl.ds(pl.multiple_of(self.graph * 16, 16), 16)
        into[mine, :] = out[mine, :]

        def one(k, carry):
            where, device = self.peer(k)
            theirs = pl.ds(pl.multiple_of(where * 16, 16), 16)
            self.copy(out.at[theirs], into.at[mine], self.ex_sent.at[e], self.ex_got.at[e], device)
            return carry

        lax.fori_loop(1, 32, one, 0)

    def exchanged(self, e, into):
        self.wait_size(into.at[pl.ds(0, 31 * 16)], self.ex_got.at[e])
        self.wait_size(into.at[pl.ds(0, 31 * 16)], self.ex_sent.at[e])


def messages_phase(comm, proj, geometry, geometry_weight, counts, sources, arrived):
    peers = counts.shape[1]
    capacity = 64
    grid_rows, width = proj.shape
    high = geometry_weight[...].astype(BF16)
    low = (geometry_weight[...] - high.astype(F32)).astype(BF16)
    count16 = jnp.broadcast_to(counts[...].astype(F32), (16, peers)).astype(BF16)
    home = comm.graph // 2
    target = arrived.at[pl.ds(pl.multiple_of(comm.graph * capacity, capacity), capacity)]

    def compute(chip):
        start = pl.multiple_of(chip * LANES, LANES)
        at = pl.ds(start, LANES)
        slot = start + iota((1, LANES), 1)
        owner = (start + iota((peers, LANES), 1)) // capacity
        limit = mm(count16, hot(owner == iota((peers, LANES), 0)))[:1]
        live = (slot % capacity).astype(F32) < limit
        index = jnp.where(live, sources[:, at], -1)
        shape = jnp.where(live, geometry[:, at].astype(F32), 0.0).astype(BF16)
        table = jnp.concatenate(row_hot(index, grid_rows), axis=1)
        pre = mm(table, proj[...]) + mm_tn(shape, high) + mm_tn(shape, low)
        where = (chip // 4, pl.ds(pl.multiple_of(lax.rem(chip, 4) * LANES, LANES), LANES))
        comm.grads[where[0], where[1], :] = (pre * sigmoid(pre)).astype(BF16)

    def part(chip, core):
        base = lax.rem(chip, 4) * LANES + core * capacity
        return comm.grads.at[chip // 4, pl.ds(pl.multiple_of(base, capacity), capacity)]

    def send(chip, core):
        comm.copy(
            part(chip, core), target, comm.ex_sent.at[4], comm.ex_got.at[4], (chip * 2 + core, comm.dp)
        )

    def step(k, carry):
        chip = lax.rem(home + k, 16)
        compute(chip)
        send(chip, 0)
        send(chip, 1)
        return carry

    lax.fori_loop(1, 16, step, 0)
    compute(home)
    send(home, 1 - comm.core)
    target[...] = part(home, comm.core)[...]


def tables_phase(senders, receivers, gather, scatter, extended):
    edges = senders.shape[1]
    nodes = gather.shape[1] - extended

    def step(i, carry):
        at = rows(i, LANES)
        send, recv = senders[:, at], receivers[:, at]
        gather[at, :extended] = jnp.concatenate(row_hot(send, extended), axis=1)
        gather[at, extended:] = jnp.concatenate(row_hot(recv, nodes), axis=1)
        scatter[:extended, at] = hot(iota((extended, LANES), 0) == send)
        scatter[extended:, at] = hot(iota((nodes, LANES), 0) == recv)
        return carry

    lax.fori_loop(0, edges // LANES, step, 0)


def halo_send(comm, e, nodes, picked, out, into):
    pack(mm(picked[...], nodes[...]).astype(BF16), out)
    comm.exchange(e, out, into)


def start_phase(arrived, targets, embed, message_weight, update, output, nodes, total):
    slots = targets.shape[1]
    count, width = embed.shape
    total[...] = jnp.zeros_like(total)

    def step(i, carry):
        at = rows(i, 2 * TILE)
        total[...] += mm(hot(iota((count, 2 * TILE), 0) == targets[:, at]), arrived[at, :])
        return carry

    lax.fori_loop(0, slots // (2 * TILE), step, 0)
    aggregate = mm(total[...].astype(BF16), message_weight[...]).astype(BF16)
    pre = mm(embed[...], update[0]) + mm(aggregate, update[1])
    normed, _ = normalize(mm((pre * sigmoid(pre)).astype(BF16), output[...]))
    nodes[...] = (embed[...].astype(F32) + normed).astype(BF16)


def forward_phase(comm, e, w, nodes, incoming, edges, gather, scatter, saved, new_nodes, proj, total, before):
    count, width = nodes.shape
    extended = gather.shape[1] - count
    proj[:count] = mm(nodes[...], w(WS)).astype(BF16)
    proj[extended:] = mm(nodes[...], w(WR)).astype(BF16)

    def early(i, carry):
        at = rows(i, TILE)
        before[at, :] = (
            mm(edges[at, :], w(WE))
            + mm(gather[at, :count], proj[:count])
            + mm(gather[at, extended:], proj[extended:])
        )
        return carry

    lax.fori_loop(0, edges.shape[0] // TILE, early, 0)
    comm.exchanged(e, incoming)
    proj[count:extended] = mm(unpack(incoming, width), w(WS)).astype(BF16)
    total[...] = jnp.zeros_like(total)

    def step(i, carry):
        at = rows(i, TILE)
        pre = before[at, :] + mm(gather[at, count:extended], proj[count:extended])
        s = sigmoid(pre)
        act = pre * s
        hid = act.astype(BF16)
        saved["hid"][at, :] = hid
        saved["slope"][at, :] = (s + act * (1.0 - s)).astype(BF16)
        normed, inverse = normalize(mm(hid, w(E2)))
        saved["normed"][at, :] = normed.astype(BF16)
        saved["inverse"][0][at, saved["inverse"][1]] = jnp.broadcast_to(inverse, (TILE, LANES // 2))
        new = (edges[at, :].astype(F32) + normed).astype(BF16)
        if saved["edges"] is not None:
            saved["edges"][at, :] = new
        total[...] += mm(scatter[extended:, at], new)
        return carry

    lax.fori_loop(0, edges.shape[0] // TILE, step, 0)
    summed = total[...].astype(BF16)
    pre = mm(nodes[...], w(PV)) + mm(summed, w(PA))
    s = sigmoid(pre)
    act = pre * s
    hid = act.astype(BF16)
    normed, inverse = normalize(mm(hid, w(N2)))
    new_nodes[...] = (nodes[...].astype(F32) + normed).astype(BF16)
    saved["summed"][...] = summed
    saved["node_hid"][...] = hid
    saved["node_slope"][...] = s + act * (1.0 - s)
    saved["node_normed"][...] = normed
    saved["node_inverse"][...] = jnp.broadcast_to(inverse, (count, LANES))


def backward_nodes(put, w, nodes, saved, grad_nodes, proj, extended):
    upstream = grad_nodes[...]
    q = normalize_back(saved["node_normed"][...], saved["node_inverse"][:, :1], upstream)
    q = q.astype(BF16)
    d_node = (mm_nt(q, w(N2)) * saved["node_slope"][...]).astype(BF16)
    proj[extended:] = mm_nt(d_node, w(PA)).astype(BF16)
    put(N2, mm_tn(saved["node_hid"][...], q))
    put(PV, mm_tn(nodes[...], d_node))
    put(PA, mm_tn(saved["summed"][...], d_node))
    grad_nodes[...] = upstream + mm_nt(d_node, w(PV))


def backward_edges(w, edges, gather, scatter, saved, grad_edges, first, last, proj, total, acc, extended, low, high):
    width = edges.shape[1]

    def step(i, carry):
        at = rows(i, TILE)
        up = mm(gather[at, extended:], proj[extended:])
        if not first:
            up = up + grad_edges[at, :]
        inverse = saved["inverse"][0][at, saved["inverse"][1]][:, :1]
        q = normalize_back(saved["normed"][at, :].astype(F32), inverse, up)
        q = q.astype(BF16)
        acc[width:] += mm_tn(saved["hid"][at, :], q)
        d = (mm_nt(q, w(E2)) * saved["slope"][at, :].astype(F32)).astype(BF16)
        acc[:width] += mm_tn(edges[at, :], d)
        total[...] += mm(scatter[:, at], d)
        if not last:
            grad_edges[at, :] = up + mm_nt(d, w(WE))
        return carry

    lax.fori_loop(low, high, step, 0)


SAVED = ("hid", "slope", "normed", "edges", "summed", "node_hid", "node_slope", "node_normed", "node_inverse")


def saved_shapes(edges, nodes, width, with_edges):
    shapes = {
        "hid": ((edges, width), BF16),
        "slope": ((edges, width), BF16),
        "normed": ((edges, width), BF16),
        "edges": ((edges, width), BF16),
        "summed": ((nodes, width), BF16),
        "node_hid": ((nodes, width), BF16),
        "node_slope": ((nodes, width), F32),
        "node_normed": ((nodes, width), F32),
        "node_inverse": ((nodes, LANES), F32),
    }
    return [shapes[name] for name in SAVED if with_edges or name != "edges"]


def saved_refs(refs, with_edges):
    names = [name for name in SAVED if with_edges or name != "edges"]
    found = dict(zip(names, refs))
    found.setdefault("edges", None)
    return found


def whole_kernel(
    scale,
    embed, geometry, counts, sources, targets, halo, senders, receivers, geometry_weight, cotangent,
    grid_any, grid_weight_any, message_weight_any, update_any, output_any, edges_any, weights_any,
    nodes2, mesh_gradient, result, *scratch,
):
    scratch = list(scratch)
    take = lambda n: [scratch.pop(0) for _ in range(n)]
    grads, half_in, quarter_in, tile_in, sent, got, ex_sent, ex_got, load = take(9)
    comm = Comm((grads, result, half_in, quarter_in, tile_in, sent, got, ex_sent, ex_got))
    arrived, edges, weights, gather, scatter, picked, nodes0, nodes1 = take(8)
    outs, ins = take(4), take(4)
    grad_edges, grad_nodes, proj, total, summing, acc = take(6)
    saved0 = saved_refs(take(len(SAVED)), True)
    saved1 = saved_refs(take(len(SAVED) - 1), False)
    (inverses,) = take(1)
    saved0["inverse"] = (inverses, slice(0, LANES // 2))
    saved1["inverse"] = (inverses, slice(LANES // 2, LANES))
    count, width = embed.shape
    extended = count + halo.shape[1]
    tiles = edges.shape[0] // TILE
    loads = [
        pltpu.make_async_copy(source, target, load.at[i])
        for i, (source, target) in enumerate(
            (
                (grid_any, grads.at[4]),
                (grid_weight_any, grads.at[5]),
                (message_weight_any, grads.at[6]),
                (output_any, grads.at[7]),
                (update_any, grads.at[pl.ds(8, 2)]),
                (edges_any, edges),
                (weights_any, weights),
            )
        )
    ]
    for copy in loads:
        copy.start()
    comm.greet()
    loads[0].wait()
    loads[1].wait()
    slots_proj = proj.at[pl.ds(0, grid_any.shape[0])]
    slots_proj[...] = mm(grads[4], grads[5]).astype(BF16)
    comm.greeted()
    messages_phase(comm, slots_proj, geometry, geometry_weight, counts, sources, arrived)
    tables_phase(senders, receivers, gather, scatter, extended)
    picked[...] = jnp.concatenate(row_hot(halo[...], count), axis=1)
    for copy in loads[2:]:
        copy.wait()
    comm.wait_size(arrived.at[pl.ds(0, 31 * 64)], ex_got.at[4])
    comm.wait_size(arrived.at[pl.ds(0, 31 * 64)], ex_sent.at[4])
    start_phase(arrived, targets, embed, grads.at[6], grads.at[pl.ds(8, 2)], grads.at[7], nodes0, summing)
    halo_send(comm, 0, nodes0, picked, outs[0], ins[0])

    def w0(which):
        return weights[block(which, width), :]

    def w1(which):
        return weights[block(7 + which, width), :]

    forward_phase(comm, 0, w0, nodes0, ins[0], edges, gather, scatter, saved0, nodes1, proj, summing, grad_edges)
    halo_send(comm, 1, nodes1, picked, outs[1], ins[1])
    edges1 = saved0["edges"]
    forward_phase(comm, 1, w1, nodes1, ins[1], edges1, gather, scatter, saved1, nodes2, proj, summing, grad_edges)
    grad_nodes[...] = cotangent[...].astype(F32)

    def putter(layer):
        def put(which, value):
            grads[layer * 7 + which] = (value * scale).astype(BF16)

        return put

    def blocks(layer, *which):
        return [layer * 7 + i for i in which]

    def clear():
        total[...] = jnp.zeros_like(total)
        acc[...] = jnp.zeros_like(acc)

    def edge_sums(put, w, nodes, e):
        pack(total[count:extended].astype(BF16), outs[e])
        comm.exchange(e, outs[e], ins[e])
        put(WE, acc[:width])
        put(E2, acc[width:])
        recv = total[extended:].astype(BF16)
        put(WR, mm_tn(nodes[...], recv))
        grad_nodes[...] += mm_nt(recv, w(WR))

    def finish(put, w, nodes, e):
        comm.exchanged(e, ins[e])
        back = hot(iota((count, halo.shape[1]), 0) == halo[...])
        send = (total[:count] + mm(back, unpack(ins[e], width))).astype(BF16)
        put(WS, mm_tn(nodes[...], send))
        grad_nodes[...] += mm_nt(send, w(WS))

    run = comm.run
    put1, put0 = putter(1), putter(0)
    backward_nodes(put1, w1, nodes1, saved1, grad_nodes, proj, extended)
    a1, b1, c1 = blocks(1, N2, PV, PA), blocks(1, WE, E2, WR), blocks(1, WS)
    a0, b0, c0 = blocks(0, N2, PV, PA), blocks(0, WE, E2, WR), blocks(0, WS)
    run(0, a1)
    clear()
    some = functools.partial(
        backward_edges, w1, edges1, gather, scatter, saved1, grad_edges, True, False, proj, total, acc, extended
    )
    some(0, tiles // 2)
    run(1, a1)
    some(tiles // 2, tiles)
    edge_sums(put1, w1, nodes1, 2)
    run(0, b1)
    run(2, a1)
    finish(put1, w1, nodes1, 2)
    run(0, c1)
    backward_nodes(put0, w0, nodes0, saved0, grad_nodes, proj, extended)
    run(0, a0)
    run(1, b1)
    run(3, a1)
    clear()
    some = functools.partial(
        backward_edges, w0, edges, gather, scatter, saved0, grad_edges, False, True, proj, total, acc, extended
    )
    some(0, tiles // 2)
    run(1, c1 + a0)
    run(2, b1)
    run(4, a1)
    some(tiles // 2, tiles)
    edge_sums(put0, w0, nodes0, 3)
    run(0, b0)
    run(2, c1 + a0)
    run(3, b1)
    run(5, a1)
    finish(put0, w0, nodes0, 3)
    run(0, c0)
    mesh_gradient[...] = grad_nodes[...].astype(BF16)
    run(1, b0)
    run(3, c1 + a0)
    run(4, b1)
    run(1, c0)
    run(2, b0)
    run(4, c1 + a0)
    run(5, b1)
    run(2, c0)
    run(3, b0)
    run(5, c1 + a0)
    run(3, c0)
    run(4, b0)
    run(4, c0)
    run(5, b0)
    run(5, c0)
    run(6, range(14))
    for b in range(14):
        comm.leave(b)


def on_device(
    grid_latent,
    mesh_embed,
    mesh_edges,
    edge_geometry,
    edge_counts,
    edge_sources,
    edge_targets,
    halo_sources,
    mesh_sources,
    mesh_targets,
    grid_weight,
    geometry_weight,
    message_weight,
    mesh_update,
    mesh_output,
    processor,
    cotangent,
):
    count, width = mesh_embed.shape
    edges = mesh_edges.shape[0]
    slots = edge_sources.shape[1]
    halo = halo_sources.shape[1]
    peers = lax.axis_size("graph")
    extended = count + halo
    table = extended + count
    tiles = (halo * width // LANES, LANES)
    scale = 1.0 / math.sqrt(lax.axis_size("dp") * peers * count)
    layers = processor.shape[0]
    vmem, anywhere = pl.BlockSpec(memory_space=pltpu.VMEM), pl.BlockSpec(memory_space=pl.ANY)
    dma = pltpu.SemaphoreType.DMA
    scratch = [
        ((7 * layers, width, width), BF16),
        ((7 * layers, width // 2, width), BF16),
        ((7 * layers, 3, width // 8, width), BF16),
        ((7 * layers, 15, 16, LANES), BF16),
        dma((7 * layers, 6)),
        dma((7 * layers, 6)),
        dma((5,)),
        dma((5,)),
        dma((7,)),
        ((slots, width), BF16),
        ((edges, width), BF16),
        ((7 * layers * width, width), BF16),
        ((edges, table), BF16),
        ((table, edges), BF16),
        ((halo, count), BF16),
        ((count, width), BF16),
        ((count, width), BF16),
        *[(tiles, BF16)] * 8,
        ((edges, width), F32),
        ((count, width), F32),
        ((table, width), BF16),
        ((table, width), F32),
        ((count, width), F32),
        ((2 * width, width), F32),
        *saved_shapes(edges, count, width, True),
        *saved_shapes(edges, count, width, False),
        ((edges, LANES), F32),
    ]
    nodes2, result, gradients = pl.pallas_call(
        functools.partial(whole_kernel, scale),
        out_shape=[
            jax.ShapeDtypeStruct((count, width), BF16),
            jax.ShapeDtypeStruct((count, width), BF16),
            jax.ShapeDtypeStruct((7 * layers, width, width), BF16),
        ],
        in_specs=[vmem] * 10 + [anywhere] * 7,
        out_specs=[vmem] * 3,
        scratch_shapes=[pltpu.VMEM(*item) if isinstance(item, tuple) else item for item in scratch],
        compiler_params=pltpu.CompilerParams(
            collective_id=0, has_side_effects=True, vmem_limit_bytes=67043328
        ),
    )(
        mesh_embed, edge_geometry[0], edge_counts, edge_sources, edge_targets, halo_sources, mesh_sources,
        mesh_targets, geometry_weight, cotangent[0],
        grid_latent[0], grid_weight, message_weight, mesh_update.reshape(2, width, width), mesh_output,
        mesh_edges, processor.reshape(-1, width),
    )
    return nodes2[None], result[None], gradients.reshape(processor.shape)


def solution(mesh):
    in_specs = (
        P("dp", "graph", None),
        P("graph", None),
        P("graph", None),
        P("graph", None, None),
        P("graph", None),
        P("graph", None),
        P("graph", None),
        P("graph", None),
        P("graph", None),
        P("graph", None),
        P(),
        P(),
        P(),
        P(),
        P(),
        P(),
        P("dp", "graph", None),
    )
    out_specs = (P("dp", "graph", None), P("dp", "graph", None), P())
    return jax.shard_map(
        on_device, mesh=mesh, in_specs=in_specs, out_specs=out_specs, check_vma=False
    )
```

time: 456 us -> 155 us (0.34)
  waiting for transfers between devices: 259 us -> 0 us
  blocking collectives: 76.1 us -> 0 us
  Pallas kernels: 84.4 us -> 144 us
  between operations: 14.1 us -> 0.65 us
    psum x2 -> x0, waiting for transfers between devices: 259 us -> none  [the longest x1 158 us: on_device(): whole0 = lax.psum(grads0, ('graph', 'dp'))]
    all_to_all x4 -> x0, blocking collectives: 76.1 us -> none  [on_device(): lax.all_to_all(values.reshape(peers, -1, values.shape[-1]), 'graph', spli...]
    pallas_call x7 -> x1, Pallas kernels: 84.4 us -> 144 us  [on_device(): pl.pallas_call(functools.partial(whole_kernel, scale), out_shape=[jax.Sha...]
    unnamed x6 -> x3, local copies, waits for them, and re-layouts: 2.19 us -> 9.94 us
    squeeze x1 -> x0, local copies, waits for them, and re-layouts: 6.63 us -> none  [on_device(): processor[0]]
  transfers between devices with their start and end apart: 3 -> 0, of which waited for: 2 -> 0; matrix products, arithmetic and copies ran while one was open for 2% -> 0% of each run, Pallas kernels for 7% -> 0%
where the time goes in v3:
time: 155 us
  Pallas kernels  144 us (93%)
  local copies, waits for them, and re-layouts  9.94 us (6%)
    pallas_call x1, Pallas kernels, on_device(): pl.pallas_call(functools.partial(whole_kernel, scale), out_shape=[jax.Sha...  144 us
    unnamed x3, local copies, waits for them, and re-layouts  9.94 us

profile of v3, /device:TPU:1, one launch (start us, length us, event | category | flops | bytes accessed | tf_op | source)
XLA Modules:
  0.0 154.8 jit_solution(4858298536045710882)
XLA Ops:
  0.6 144.2 %shard_map.184 = (bf16[256,512]{1,0:T(8,128)(2,1)}, bf16[256,512]{1,0:T(8,128)(2,1)}, bf16[14,512,512]{2,1,0:T(8,128)(2,1)}) custom-call(bf16[256,512]{1,0:T(8,128)(2,1)} %embed.1, bf16[4,2048]{1,0:T(4,128)(2,1)} %bitcast.15, s32[1,32]{1,0:T(1,128)} %counts.1, s32[1,2048]{1,0:T(1,128)} %sources.1, s32[1,2048]{1,0:T(1,128)} %targets.1, s32[1,128]{1,0:T(1,128)} %halo.1, ...), custom_call_target="tpu_custom_call" | custom-call | tf_op jit(solution)/shard_map/pallas_call | solution.py:678
  144.9 1.7 %copy.23 = bf16[1,256,512]{2,1,0:T(8,128)(2,1)} copy(bf16[1,256,512]{2,1,0:T(8,128)(2,1)} %bitcast.14) | data formatting | bytes 524288
  146.5 1.7 %copy.24 = bf16[1,256,512]{2,1,0:T(8,128)(2,1)} copy(bf16[1,256,512]{2,1,0:T(8,128)(2,1)} %bitcast.13) | data formatting | bytes 524288
  148.2 6.6 %copy.25 = bf16[2,3584,512]{2,1,0:T(8,128)(2,1)} copy(bf16[2,3584,512]{2,1,0:T(8,128)(2,1)} %bitcast.8) | data formatting | bytes 14680064

commit v4 on v3

--- a/solution.py
+++ b/solution.py
@@ -11,7 +11,7 @@
 EPSILON = 1e-05
 F32, BF16 = jnp.float32, jnp.bfloat16
 LANES = 128
-TILE = 256
+TILE = 512
 WE, WS, WR, E2, PV, PA, N2 = range(7)
 
 
@@ -91,7 +91,12 @@
     )
 
 
-AXES = (1, 1, 0, 2, 2, 0, 1, 0, 0, 2, 1, 1, 2, 0)
+STAGES = 8
+AXES = (0, 1, 2, 0, 2, 0, 1, 0, 1, 2, 1, 1, 2, 0)
+
+
+FIRST = ((2, 0), (0, 2), (2, 1), (1, 2), (2, 2), (3, 2), (2, 3))
+THEN = ((1, 1), (3, 1), (1, 3), (3, 3), (1, 0), (3, 0), (0, 1), (0, 3))
 
 
 class Comm:
@@ -103,6 +108,7 @@
         self.graph, self.dp = lax.axis_index("graph"), lax.axis_index("dp")
         self.core = lax.rem(self.graph, 2)
         self.place = [lax.rem(self.graph // 2, 4), self.graph // 8, self.dp]
+        self.spots = [[self.find_spot(axis, k) for k in range(16)] for axis in range(3)]
 
     def device(self, core, place):
         return (place[1] * 8 + place[0] * 2 + core, place[2])
@@ -113,6 +119,9 @@
     def peer(self, k):
         where = lax.rem(self.graph + k, 32)
         return where, (where, self.dp)
+
+    def chip(self, dx, dy):
+        return lax.rem(self.place[1] + dy, 4) * 4 + lax.rem(self.place[0] + dx, 4)
 
     def along(self, axis, k):
         place = list(self.place)
@@ -164,10 +173,10 @@
         pltpu.make_async_copy(size, size, semaphore).wait()
 
     def wait(self, semaphores, b, stage):
-        sizes = (
-            self.half_in.at[b], self.quarter_in.at[b], self.tile_in.at[b],
-            self.tile_in.at[b], self.quarter_in.at[b], self.half_in.at[b],
+        whole, half, full, tiles = (
+            self.half_in.at[b], self.quarter_in.at[b, 2], self.quarter_in.at[b, pl.ds(0, 2)], self.tile_in.at[b]
         )
+        sizes = (whole, half, full, tiles, tiles, full, half, whole)
         self.wait_size(sizes[stage], semaphores.at[b, stage])
 
     def spot(self, where):
@@ -181,74 +190,95 @@
     def quarter_rows(self, at):
         return pl.ds(pl.multiple_of(self.core * 256 + at * 64, 64), 64)
 
+    def find_spot(self, axis, k):
+        where, device = self.over(axis, k)
+        at, lane = self.spot(where)
+        return pl.multiple_of(self.core * 256 + self.place[axis] * 64 + at, 16), lane, device
+
     def own_spot(self, b, k):
-        where, device = self.over(AXES[b], k)
-        at, lane = self.spot(where)
-        base = self.core * 256 + self.place[AXES[b]] * 64
-        return (pl.ds(pl.multiple_of(base + at, 16), 16), pl.ds(lane, LANES)), device
+        at, lane, device = self.spots[AXES[b]][k]
+        return (pl.ds(at, 16), pl.ds(lane, LANES)), device
 
     def begin(self, b):
         other = self.half_rows(1 - self.core)
         self.send(b, 0, self.grads.at[b, other], self.half_in.at[b], self.partner())
+
+    def part(self, b, k, half):
+        base = self.core * 256 + self.along(AXES[b], k)[0] * 64
+        size = 64 if half is None else 32
+        return pl.ds(pl.multiple_of(base + (32 if half == 1 else 0), size), size)
 
     def step1(self, b):
         self.wait(self.got, b, 0)
         mine = self.half_rows(self.core)
         self.grads[b, mine, :] = (self.grads[b, mine, :].astype(F32) + self.half_in[b].astype(F32)).astype(BF16)
-        for k in range(1, 4):
-            at, device = self.along(AXES[b], k)
-            self.send(b, 1, self.grads.at[b, self.quarter_rows(at)], self.quarter_in.at[b, k - 1], device)
+        for half, k in ((0, 1), (1, 3)):
+            target = self.quarter_in.at[b, 2, pl.ds(half * 32, 32)]
+            self.send(b, 1, self.grads.at[b, self.part(b, 2, half)], target, self.along(AXES[b], k)[1])
 
     def step2(self, b):
         self.wait(self.got, b, 1)
-        mine = self.quarter_rows(self.place[AXES[b]])
+        for half, k in ((0, 1), (1, 3)):
+            mine = self.part(b, k, half)
+            more = self.quarter_in[b, 2, pl.ds(half * 32, 32), :].astype(F32)
+            self.grads[b, mine, :] = (self.grads[b, mine, :].astype(F32) + more).astype(BF16)
+            self.send(
+                b, 2, self.grads.at[b, self.part(b, k, None)], self.quarter_in.at[b, half], self.along(AXES[b], k)[1]
+            )
+
+    def step3(self, b):
+        self.wait(self.got, b, 2)
+        mine = self.part(b, 0, None)
         total = self.grads[b, mine, :].astype(F32)
-        for k in range(3):
+        for k in range(2):
             total = total + self.quarter_in[b, k].astype(F32)
         self.grads[b, mine, :] = total.astype(BF16)
 
-        def one(k, carry):
+        for k in range(1, 16):
             spot, device = self.own_spot(b, k)
-            self.send(b, 2, self.grads.at[b, spot[0], spot[1]], self.tile_in.at[b, k - 1], device)
-            return carry
-
-        lax.fori_loop(1, 16, one, 0)
-
-    def step3(self, b):
-        self.wait(self.got, b, 2)
+            self.send(b, 3, self.grads.at[b, spot[0], spot[1]], self.tile_in.at[b, k - 1], device)
+
+    def step4(self, b):
+        self.wait(self.got, b, 3)
         spot, _ = self.own_spot(b, 0)
         total = self.grads[b, spot[0], spot[1]].astype(F32)
         total = total + jnp.sum(self.tile_in[b].astype(F32), axis=0)
         mine = self.result.at[b, spot[0], spot[1]]
         mine[...] = total.astype(BF16)
 
-        def one(k, carry):
-            self.send(b, 3, mine, mine, self.over(AXES[b], k)[1])
-            return carry
-
-        lax.fori_loop(1, 16, one, 0)
-
-    def step4(self, b):
-        self.wait(self.got, b, 3)
-        mine = self.result.at[b, self.quarter_rows(self.place[AXES[b]])]
-        for k in range(1, 4):
-            self.send(b, 4, mine, mine, self.along(AXES[b], k)[1])
+        for k in range(1, 16):
+            self.send(b, 4, mine, mine, self.own_spot(b, k)[1])
 
     def step5(self, b):
         self.wait(self.got, b, 4)
-        mine = self.result.at[b, self.half_rows(self.core)]
-        self.send(b, 5, mine, mine, self.partner())
+        mine = self.result.at[b, self.part(b, 0, None)]
+        for k in (1, 3):
+            self.send(b, 5, mine, mine, self.along(AXES[b], k)[1])
 
     def step6(self, b):
         self.wait(self.got, b, 5)
+        for half, k in ((0, 1), (1, 3)):
+            other = self.result.at[b, self.part(b, 4 - k, half)]
+            self.send(b, 6, other, other, self.along(AXES[b], k)[1])
+
+    def step7(self, b):
+        self.wait(self.got, b, 6)
+        mine = self.result.at[b, self.half_rows(self.core)]
+        self.send(b, 7, mine, mine, self.partner())
+
+    def step8(self, b):
+        self.wait(self.got, b, 7)
 
     def leave(self, b):
-        for stage in range(6):
+        for stage in range(STAGES):
             self.wait(self.sent, b, stage)
 
     def run(self, step, blocks):
+        steps = (
+            self.begin, self.step1, self.step2, self.step3, self.step4, self.step5, self.step6, self.step7, self.step8
+        )
         for b in blocks:
-            (self.begin, self.step1, self.step2, self.step3, self.step4, self.step5, self.step6)[step](b)
+            steps[step](b)
 
     def exchange(self, e, out, into):
         mine = pl.ds(pl.multiple_of(self.graph * 16, 16), 16)
@@ -300,14 +330,11 @@
             part(chip, core), target, comm.ex_sent.at[4], comm.ex_got.at[4], (chip * 2 + core, comm.dp)
         )
 
-    def step(k, carry):
-        chip = lax.rem(home + k, 16)
+    for dx, dy in FIRST + THEN:
+        chip = comm.chip(dx, dy)
         compute(chip)
-        send(chip, 0)
-        send(chip, 1)
-        return carry
-
-    lax.fori_loop(1, 16, step, 0)
+        send(chip, 1 - comm.core)
+        send(chip, comm.core)
     compute(home)
     send(home, 1 - comm.core)
     target[...] = part(home, comm.core)[...]
@@ -340,11 +367,11 @@
     total[...] = jnp.zeros_like(total)
 
     def step(i, carry):
-        at = rows(i, 2 * TILE)
-        total[...] += mm(hot(iota((count, 2 * TILE), 0) == targets[:, at]), arrived[at, :])
+        at = rows(i, TILE)
+        total[...] += mm(hot(iota((count, TILE), 0) == targets[:, at]), arrived[at, :])
         return carry
 
-    lax.fori_loop(0, slots // (2 * TILE), step, 0)
+    lax.fori_loop(0, slots // TILE, step, 0)
     aggregate = mm(total[...].astype(BF16), message_weight[...]).astype(BF16)
     pre = mm(embed[...], update[0]) + mm(aggregate, update[1])
     normed, _ = normalize(mm((pre * sigmoid(pre)).astype(BF16), output[...]))
@@ -415,9 +442,7 @@
     grad_nodes[...] = upstream + mm_nt(d_node, w(PV))
 
 
-def backward_edges(w, edges, gather, scatter, saved, grad_edges, first, last, proj, total, acc, extended, low, high):
-    width = edges.shape[1]
-
+def backward_inner(gather, saved, grad_edges, first, last, proj, acc, extended, low, high):
     def step(i, carry):
         at = rows(i, TILE)
         up = mm(gather[at, extended:], proj[extended:])
@@ -426,12 +451,23 @@
         inverse = saved["inverse"][0][at, saved["inverse"][1]][:, :1]
         q = normalize_back(saved["normed"][at, :].astype(F32), inverse, up)
         q = q.astype(BF16)
-        acc[width:] += mm_tn(saved["hid"][at, :], q)
-        d = (mm_nt(q, w(E2)) * saved["slope"][at, :].astype(F32)).astype(BF16)
-        acc[:width] += mm_tn(edges[at, :], d)
+        acc[...] += mm_tn(saved["hid"][at, :], q)
+        saved["hid"][at, :] = q
+        if not last:
+            grad_edges[at, :] = up
+        return carry
+
+    lax.fori_loop(low, high, step, 0)
+
+
+def backward_outer(w, edges, scatter, saved, grad_edges, last, total, acc, low, high):
+    def step(i, carry):
+        at = rows(i, TILE)
+        d = (mm_nt(saved["hid"][at, :], w(E2)) * saved["slope"][at, :].astype(F32)).astype(BF16)
+        acc[...] += mm_tn(edges[at, :], d)
         total[...] += mm(scatter[:, at], d)
         if not last:
-            grad_edges[at, :] = up + mm_nt(d, w(WE))
+            grad_edges[at, :] += mm_nt(d, w(WE))
         return carry
 
     lax.fori_loop(low, high, step, 0)
@@ -474,7 +510,7 @@
     comm = Comm((grads, result, half_in, quarter_in, tile_in, sent, got, ex_sent, ex_got))
     arrived, edges, weights, gather, scatter, picked, nodes0, nodes1 = take(8)
     outs, ins = take(4), take(4)
-    grad_edges, grad_nodes, proj, total, summing, acc = take(6)
+    grad_edges, grad_nodes, proj, total, summing, acc_inner, acc_outer = take(7)
     saved0 = saved_refs(take(len(SAVED)), True)
     saved1 = saved_refs(take(len(SAVED) - 1), False)
     (inverses,) = take(1)
@@ -511,7 +547,6 @@
     for copy in loads[2:]:
         copy.wait()
     comm.wait_size(arrived.at[pl.ds(0, 31 * 64)], ex_got.at[4])
-    comm.wait_size(arrived.at[pl.ds(0, 31 * 64)], ex_sent.at[4])
     start_phase(arrived, targets, embed, grads.at[6], grads.at[pl.ds(8, 2)], grads.at[7], nodes0, summing)
     halo_send(comm, 0, nodes0, picked, outs[0], ins[0])
 
@@ -538,79 +573,111 @@
 
     def clear():
         total[...] = jnp.zeros_like(total)
-        acc[...] = jnp.zeros_like(acc)
-
-    def edge_sums(put, w, nodes, e):
-        pack(total[count:extended].astype(BF16), outs[e])
+        acc_inner[...] = jnp.zeros_like(acc_inner)
+        acc_outer[...] = jnp.zeros_like(acc_outer)
+
+    def edge_sums(put, w, nodes, e, incoming):
+        outer = total[count:extended].astype(BF16)
+        pack(outer, outs[e])
         comm.exchange(e, outs[e], ins[e])
-        put(WE, acc[:width])
-        put(E2, acc[width:])
+        put(WE, acc_outer[...])
         recv = total[extended:].astype(BF16)
         put(WR, mm_tn(nodes[...], recv))
+        put(WS, mm_tn(nodes[...], total[:count].astype(BF16)) + mm_tn(unpack(incoming, width), outer))
         grad_nodes[...] += mm_nt(recv, w(WR))
 
-    def finish(put, w, nodes, e):
+    def finish(w, e):
         comm.exchanged(e, ins[e])
         back = hot(iota((count, halo.shape[1]), 0) == halo[...])
         send = (total[:count] + mm(back, unpack(ins[e], width))).astype(BF16)
-        put(WS, mm_tn(nodes[...], send))
         grad_nodes[...] += mm_nt(send, w(WS))
 
     run = comm.run
     put1, put0 = putter(1), putter(0)
+    a1, e1, b1 = blocks(1, N2, PV, PA), blocks(1, E2), blocks(1, WE, WR, WS)
+    a0, e0, b0 = blocks(0, N2, PV, PA), blocks(0, E2), blocks(0, WE, WR, WS)
+    comm.wait_size(arrived.at[pl.ds(0, 31 * 64)], ex_sent.at[4])
+
+    pieces = [(i * tiles // 3, (i + 1) * tiles // 3) for i in range(3)]
+
+    def inner(piece, saved, first, last):
+        backward_inner(gather, saved, grad_edges, first, last, proj, acc_inner, extended, *pieces[piece])
+
+    def outer(piece, w, edges, saved, last):
+        backward_outer(w, edges, scatter, saved, grad_edges, last, total, acc_outer, *pieces[piece])
+
+    clear()
     backward_nodes(put1, w1, nodes1, saved1, grad_nodes, proj, extended)
-    a1, b1, c1 = blocks(1, N2, PV, PA), blocks(1, WE, E2, WR), blocks(1, WS)
-    a0, b0, c0 = blocks(0, N2, PV, PA), blocks(0, WE, E2, WR), blocks(0, WS)
     run(0, a1)
+    inner(0, saved1, True, False)
+    inner(1, saved1, True, False)
+    inner(2, saved1, True, False)
+    put1(E2, acc_inner[...])
+    run(0, e1)
+    run(1, a1)
+    outer(0, w1, edges1, saved1, False)
+    outer(1, w1, edges1, saved1, False)
+    run(1, e1)
+    outer(2, w1, edges1, saved1, False)
+    run(2, a1)
+    edge_sums(put1, w1, nodes1, 2, ins[1])
+    run(0, b1)
+    run(2, e1)
+    finish(w1, 2)
+    run(3, a1)
     clear()
-    some = functools.partial(
-        backward_edges, w1, edges1, gather, scatter, saved1, grad_edges, True, False, proj, total, acc, extended
-    )
-    some(0, tiles // 2)
-    run(1, a1)
-    some(tiles // 2, tiles)
-    edge_sums(put1, w1, nodes1, 2)
-    run(0, b1)
-    run(2, a1)
-    finish(put1, w1, nodes1, 2)
-    run(0, c1)
     backward_nodes(put0, w0, nodes0, saved0, grad_nodes, proj, extended)
     run(0, a0)
     run(1, b1)
-    run(3, a1)
-    clear()
-    some = functools.partial(
-        backward_edges, w0, edges, gather, scatter, saved0, grad_edges, False, True, proj, total, acc, extended
-    )
-    some(0, tiles // 2)
-    run(1, c1 + a0)
+    run(3, e1)
+    inner(0, saved0, False, True)
+    inner(1, saved0, False, True)
+    inner(2, saved0, False, True)
+    put0(E2, acc_inner[...])
+    run(0, e0)
+    run(1, a0)
+    run(4, a1)
+    outer(0, w0, edges, saved0, True)
     run(2, b1)
-    run(4, a1)
-    some(tiles // 2, tiles)
-    edge_sums(put0, w0, nodes0, 3)
+    run(4, e1)
+    outer(1, w0, edges, saved0, True)
+    run(1, e0)
+    outer(2, w0, edges, saved0, True)
+    run(2, a0)
+    edge_sums(put0, w0, nodes0, 3, ins[0])
     run(0, b0)
-    run(2, c1 + a0)
+    run(5, a1)
+    run(5, e1)
     run(3, b1)
-    run(5, a1)
-    finish(put0, w0, nodes0, 3)
-    run(0, c0)
+    run(2, e0)
+    run(1, b0)
+    run(3, a0)
+    finish(w0, 3)
     mesh_gradient[...] = grad_nodes[...].astype(BF16)
-    run(1, b0)
-    run(3, c1 + a0)
+    run(2, b0)
     run(4, b1)
-    run(1, c0)
-    run(2, b0)
-    run(4, c1 + a0)
+    run(3, e0)
+    run(6, a1)
+    run(6, e1)
+    run(3, b0)
+    run(4, a0)
+    run(4, e0)
+    run(7, a1)
+    run(7, e1)
     run(5, b1)
-    run(2, c0)
-    run(3, b0)
-    run(5, c1 + a0)
-    run(3, c0)
     run(4, b0)
-    run(4, c0)
+    run(5, a0)
+    run(5, e0)
+    run(6, b1)
     run(5, b0)
-    run(5, c0)
-    run(6, range(14))
+    run(6, a0)
+    run(6, e0)
+    run(7, b1)
+    run(6, b0)
+    run(7, a0)
+    run(7, e0)
+    run(7, b0)
+    run(8, range(14))
     for b in range(14):
         comm.leave(b)
 
@@ -651,8 +718,8 @@
         ((7 * layers, width // 2, width), BF16),
         ((7 * layers, 3, width // 8, width), BF16),
         ((7 * layers, 15, 16, LANES), BF16),
-        dma((7 * layers, 6)),
-        dma((7 * layers, 6)),
+        dma((7 * layers, STAGES)),
+        dma((7 * layers, STAGES)),
         dma((5,)),
         dma((5,)),
         dma((7,)),
@@ -670,7 +737,8 @@
         ((table, width), BF16),
         ((table, width), F32),
         ((count, width), F32),
-        ((2 * width, width), F32),
+        ((width, width), F32),
+        ((width, width), F32),
         *saved_shapes(edges, count, width, True),
         *saved_shapes(edges, count, width, False),
         ((edges, LANES), F32),
@@ -678,15 +746,15 @@
     nodes2, result, gradients = pl.pallas_call(
         functools.partial(whole_kernel, scale),
         out_shape=[
-            jax.ShapeDtypeStruct((count, width), BF16),
-            jax.ShapeDtypeStruct((count, width), BF16),
-            jax.ShapeDtypeStruct((7 * layers, width, width), BF16),
+            pltpu.VMEM((count, width), BF16),
+            pltpu.VMEM((count, width), BF16),
+            pltpu.VMEM((7 * layers, width, width), BF16),
         ],
         in_specs=[vmem] * 10 + [anywhere] * 7,
         out_specs=[vmem] * 3,
         scratch_shapes=[pltpu.VMEM(*item) if isinstance(item, tuple) else item for item in scratch],
         compiler_params=pltpu.CompilerParams(
-            collective_id=0, has_side_effects=True, vmem_limit_bytes=67043328
+            collective_id=0, has_side_effects=True, vmem_limit_bytes=59100000
         ),
     )(
         mesh_embed, edge_geometry[0], edge_counts, edge_sources, edge_targets, halo_sources, mesh_sources,

time: 155 us -> 134 us (0.86)
  Pallas kernels: 144 us -> 129 us
  local copies, waits for them, and re-layouts: 9.94 us -> 4.45 us
    pallas_call x1, Pallas kernels: 144 us -> 129 us  [on_device(): pl.pallas_call(functools.partial(whole_kernel, scale), out_shape=[pltpu.V...]
    unnamed x3, local copies, waits for them, and re-layouts: 9.94 us -> 4.45 us
where the time goes in v4:
time: 134 us
  Pallas kernels  129 us (96%)
  local copies, waits for them, and re-layouts  4.45 us (3%)
    pallas_call x1, Pallas kernels, on_device(): pl.pallas_call(functools.partial(whole_kernel, scale), out_shape=[pltpu.V...  129 us
    unnamed x3, local copies, waits for them, and re-layouts  4.45 us

profile of v4, /device:TPU:1, one launch (start us, length us, event | category | flops | bytes accessed | tf_op | source)
XLA Modules:
  0.0 134.2 jit_solution(15665294620339534481)
XLA Ops:
  0.6 129.1 %shard_map.184 = (bf16[256,512]{1,0:T(8,128)(2,1)S(1)}, bf16[256,512]{1,0:T(8,128)(2,1)S(1)}, bf16[14,512,512]{2,1,0:T(8,128)(2,1)S(1)}) custom-call(bf16[256,512]{1,0:T(8,128)(2,1)} %embed.1, bf16[4,2048]{1,0:T(4,128)(2,1)} %bitcast.15, s32[1,32]{1,0:T(1,128)} %counts.1, s32[1,2048]{1,0:T(1,128)} %sources.1, s32[1,2048]{1,0:T(1,128)} %targets.1, ...), custom_call_target="tpu_custom_call" | custom-call | tf_op jit(solution)/shard_map/pallas_call | solution.py:746
  129.7 0.7 copy.23
  130.4 0.7 copy.24
  131.1 3.0 %copy.25 = bf16[2,3584,512]{2,1,0:T(8,128)(2,1)} copy(bf16[2,3584,512]{2,1,0:T(8,128)(2,1)S(1)} %bitcast.8) | data formatting | bytes 14680064

commit v5 on v4

--- a/solution.py
+++ b/solution.py
@@ -460,14 +460,26 @@
     lax.fori_loop(low, high, step, 0)
 
 
-def backward_outer(w, edges, scatter, saved, grad_edges, last, total, acc, low, high):
+def backward_outer(w, edges, scatter, saved, total, acc, low, high):
     def step(i, carry):
         at = rows(i, TILE)
         d = (mm_nt(saved["hid"][at, :], w(E2)) * saved["slope"][at, :].astype(F32)).astype(BF16)
+        total[...] += mm(scatter[:, at], d)
+        if acc is None:
+            saved["hid"][at, :] = d
+        else:
+            acc[...] += mm_tn(edges[at, :], d)
+        return carry
+
+    lax.fori_loop(low, high, step, 0)
+
+
+def backward_rest(w, edges, saved, grad_edges, acc, low, high):
+    def step(i, carry):
+        at = rows(i, TILE)
+        d = saved["hid"][at, :]
         acc[...] += mm_tn(edges[at, :], d)
-        total[...] += mm(scatter[:, at], d)
-        if not last:
-            grad_edges[at, :] += mm_nt(d, w(WE))
+        grad_edges[at, :] += mm_nt(d, w(WE))
         return carry
 
     lax.fori_loop(low, high, step, 0)
@@ -533,11 +545,13 @@
             )
         )
     ]
-    for copy in loads:
+    for copy in loads[:2]:
         copy.start()
     comm.greet()
-    loads[0].wait()
-    loads[1].wait()
+    for copy in loads[:2]:
+        copy.wait()
+    for copy in loads[2:]:
+        copy.start()
     slots_proj = proj.at[pl.ds(0, grid_any.shape[0])]
     slots_proj[...] = mm(grads[4], grads[5]).astype(BF16)
     comm.greeted()
@@ -571,19 +585,24 @@
     def blocks(layer, *which):
         return [layer * 7 + i for i in which]
 
+    run = comm.run
+
     def clear():
         total[...] = jnp.zeros_like(total)
         acc_inner[...] = jnp.zeros_like(acc_inner)
         acc_outer[...] = jnp.zeros_like(acc_outer)
 
-    def edge_sums(put, w, nodes, e, incoming):
-        outer = total[count:extended].astype(BF16)
-        pack(outer, outs[e])
+    def give_back(e):
+        pack(total[count:extended].astype(BF16), outs[e])
         comm.exchange(e, outs[e], ins[e])
-        put(WE, acc_outer[...])
+
+    def edge_sums(put, w, nodes, layer, incoming):
         recv = total[extended:].astype(BF16)
         put(WR, mm_tn(nodes[...], recv))
-        put(WS, mm_tn(nodes[...], total[:count].astype(BF16)) + mm_tn(unpack(incoming, width), outer))
+        run(0, blocks(layer, WR))
+        outer16 = total[count:extended].astype(BF16)
+        put(WS, mm_tn(nodes[...], total[:count].astype(BF16)) + mm_tn(unpack(incoming, width), outer16))
+        run(0, blocks(layer, WS))
         grad_nodes[...] += mm_nt(recv, w(WR))
 
     def finish(w, e):
@@ -592,7 +611,6 @@
         send = (total[:count] + mm(back, unpack(ins[e], width))).astype(BF16)
         grad_nodes[...] += mm_nt(send, w(WS))
 
-    run = comm.run
     put1, put0 = putter(1), putter(0)
     a1, e1, b1 = blocks(1, N2, PV, PA), blocks(1, E2), blocks(1, WE, WR, WS)
     a0, e0, b0 = blocks(0, N2, PV, PA), blocks(0, E2), blocks(0, WE, WR, WS)
@@ -603,8 +621,11 @@
     def inner(piece, saved, first, last):
         backward_inner(gather, saved, grad_edges, first, last, proj, acc_inner, extended, *pieces[piece])
 
-    def outer(piece, w, edges, saved, last):
-        backward_outer(w, edges, scatter, saved, grad_edges, last, total, acc_outer, *pieces[piece])
+    def outer(piece, w, edges, saved, acc):
+        backward_outer(w, edges, scatter, saved, total, acc, *pieces[piece])
+
+    def rest(piece):
+        backward_rest(w1, edges1, saved1, grad_edges, acc_outer, *pieces[piece])
 
     clear()
     backward_nodes(put1, w1, nodes1, saved1, grad_nodes, proj, extended)
@@ -615,16 +636,21 @@
     put1(E2, acc_inner[...])
     run(0, e1)
     run(1, a1)
-    outer(0, w1, edges1, saved1, False)
-    outer(1, w1, edges1, saved1, False)
+    outer(0, w1, edges1, saved1, None)
+    outer(1, w1, edges1, saved1, None)
     run(1, e1)
-    outer(2, w1, edges1, saved1, False)
+    outer(2, w1, edges1, saved1, None)
     run(2, a1)
-    edge_sums(put1, w1, nodes1, 2, ins[1])
-    run(0, b1)
+    give_back(2)
     run(2, e1)
+    rest(0)
+    rest(1)
+    rest(2)
+    put1(WE, acc_outer[...])
+    run(0, blocks(1, WE))
+    edge_sums(put1, w1, nodes1, 1, ins[1])
+    run(3, a1)
     finish(w1, 2)
-    run(3, a1)
     clear()
     backward_nodes(put0, w0, nodes0, saved0, grad_nodes, proj, extended)
     run(0, a0)
@@ -637,20 +663,22 @@
     run(0, e0)
     run(1, a0)
     run(4, a1)
-    outer(0, w0, edges, saved0, True)
+    outer(0, w0, edges, saved0, acc_outer)
     run(2, b1)
     run(4, e1)
-    outer(1, w0, edges, saved0, True)
+    outer(1, w0, edges, saved0, acc_outer)
     run(1, e0)
-    outer(2, w0, edges, saved0, True)
+    outer(2, w0, edges, saved0, acc_outer)
     run(2, a0)
-    edge_sums(put0, w0, nodes0, 3, ins[0])
-    run(0, b0)
+    put0(WE, acc_outer[...])
+    run(0, blocks(0, WE))
+    edge_sums(put0, w0, nodes0, 0, ins[0])
+    give_back(3)
+    run(2, e0)
+    run(1, b0)
+    run(3, b1)
     run(5, a1)
     run(5, e1)
-    run(3, b1)
-    run(2, e0)
-    run(1, b0)
     run(3, a0)
     finish(w0, 3)
     mesh_gradient[...] = grad_nodes[...].astype(BF16)

time: 134 us -> 131 us (0.978)
  Pallas kernels: 129 us -> 126 us
    pallas_call x1, Pallas kernels: 129 us -> 126 us  [on_device(): pl.pallas_call(functools.partial(whole_kernel, scale), out_shape=[pltpu.V...]
where the time goes in v5:
time: 131 us
  Pallas kernels  126 us (96%)
  local copies, waits for them, and re-layouts  4.45 us (3%)
    pallas_call x1, Pallas kernels, on_device(): pl.pallas_call(functools.partial(whole_kernel, scale), out_shape=[pltpu.V...  126 us
    unnamed x3, local copies, waits for them, and re-layouts  4.45 us

profile of v5, /device:TPU:1, one launch (start us, length us, event | category | flops | bytes accessed | tf_op | source)
XLA Modules:
  0.0 130.8 jit_solution(15940608128674506167)
XLA Ops:
  0.6 125.6 %shard_map.184 = (bf16[256,512]{1,0:T(8,128)(2,1)S(1)}, bf16[256,512]{1,0:T(8,128)(2,1)S(1)}, bf16[14,512,512]{2,1,0:T(8,128)(2,1)S(1)}) custom-call(bf16[256,512]{1,0:T(8,128)(2,1)} %embed.1, bf16[4,2048]{1,0:T(4,128)(2,1)} %bitcast.15, s32[1,32]{1,0:T(1,128)} %counts.1, s32[1,2048]{1,0:T(1,128)} %sources.1, s32[1,2048]{1,0:T(1,128)} %targets.1, ...), custom_call_target="tpu_custom_call" | custom-call | tf_op jit(solution)/shard_map/pallas_call | solution.py:774
  126.3 0.7 copy.23
  127.0 0.7 copy.24
  127.7 3.0 %copy.25 = bf16[2,3584,512]{2,1,0:T(8,128)(2,1)} copy(bf16[2,3584,512]{2,1,0:T(8,128)(2,1)S(1)} %bitcast.8) | data formatting | bytes 14680064
